TPU v7x, 32 devices: a whole 2x2x4 slice. The times are simulated.
32 devices in a mesh: seg: 2 (over y), row: 8 (over z, x), col: 2 (over core).
Axes of the slice: x: 2, y: 2, z: 4, core: 2. Of those that a mesh axis runs over, the one named last changes fastest.
Arguments:
- slices: bfloat16 [4, 4096, 4096], P('col', 'seg', 'row'), may hold values from -1 to 1
Outputs:
- prefixes: bfloat16 [4, 4096, 4096], P('col', 'seg', 'row')
All inputs are finite; a program needn't handle non-finite values.
Results may differ from a plain program's by a relative error of at most 0.004.
Values may be sent and summed in bfloat16 or wider, within the bound.
No kernel may reach another device: no remote copies, remote signals or barrier semaphores. Data moves between devices by JAX's collectives and lax.ppermute only.
A program may use at most 128 MiB of HBM per device.

v0:
```python
import math

import jax
import jax.numpy as jnp
from jax import lax
from jax.sharding import PartitionSpec as P

ORDER = 4096


def passed_along(value, axis, by):
    count = lax.axis_size(axis)
    pairs = [(i, i + by) for i in range(count) if 0 <= i + by < count]
    return lax.ppermute(value, axis, pairs)


def column_panel(tile):
    return lax.all_gather(tile, "seg", axis=0, tiled=True)


def times_panel(left_tile, right_block):
    gathered = lax.all_gather(left_tile, "row", axis=1, tiled=True)
    return jnp.dot(gathered, right_block, preferred_element_type=jnp.float32)


def earlier_panel(tile, distance):
    return passed_along(column_panel(tile), "col", distance)


def local(slices):
    group_index = lax.axis_index("col")
    group_count = lax.axis_size("col")
    history = [slices[0]]
    history.append(times_panel(slices[1], column_panel(history[-1])).astype(jnp.bfloat16))
    running = history[-1]
    distance = 1
    while distance < group_count:
        product = times_panel(running, earlier_panel(running, distance)).astype(jnp.bfloat16)
        running = jnp.where(group_index >= distance, product, running)
        distance = distance * 2
    carried_block = earlier_panel(running, 1)
    factor = math.sqrt(ORDER)
    results = []
    for local_tile in history:
        applied = times_panel(local_tile, carried_block)
        chosen = jnp.where(group_index > 0, applied, local_tile.astype(jnp.float32))
        results.append((chosen * factor).astype(jnp.bfloat16))
    return jnp.stack(results, axis=0)


def solution(mesh):
    in_specs = (P("col", "seg", "row"),)
    out_specs = P("col", "seg", "row")
    return jax.shard_map(local, mesh=mesh, in_specs=in_specs, out_specs=out_specs, check_vma=False)
```

profile of v0, /device:TPU:0, one launch (start us, length us, event | category | flops | bytes accessed | tf_op | source)
XLA Modules:
  0.0 920.9 jit_solution(10815625901203171808)
XLA Ops:
  6.5 0.0 all-gather.18.cloned.1.call-start
  6.5 4.5 fusion.19
  11.1 0.0 all-gather.18.cloned.1.call-update
  11.1 0.0 all-gather.16.cloned.1.call-start
  11.2 0.7 all-gather.16.cloned.1.call-update
  11.9 0.0 all-gather.12.cloned.1.call-start
  11.9 58.8 %all-gather.18.cloned.1.call-done = bf16[1,4096,512]{2,1,0:T(8,128)(2,1)} async-done(((bf16[1,2048,512]{2,1,0:T(8,128)(2,1)}), bf16[1,4096,512]{2,1,0:T(8,128)(2,1)}) %all-gather.18.cloned.1.call-update) | async-done | bytes 4194320 | tf_op jit(solution)/shard_map/all_gather | solution.py:18
  70.7 229.4 %all-gather.16.cloned.1.call-done = bf16[1,2048,4096]{2,1,0:T(8,128)(2,1)} async-done(((bf16[1,2048,512]{2,1,0:T(8,128)(2,1)}), bf16[1,2048,4096]{2,1,0:T(8,128)(2,1)}) %all-gather.16.cloned.1.call-update) | async-done | bytes 16777232 | tf_op jit(solution)/shard_map/all_gather | solution.py:22
  300.1 14.5 %fusion.9 = bf16[2048,512]{1,0:T(8,128)(2,1)} fusion(bf16[1,4096,512]{2,1,0:T(8,128)(2,1)} %all-gather.18.cloned.1.call-done, bf16[1,2048,4096]{2,1,0:T(8,128)(2,1)} %all-gather.16.cloned.1.call-done), kind=kOutput, calls=%fused_computation.10 | convolution fusion | flops 8590983168 | bytes 23068672 | tf_op jit(solution)/shard_map/dot_general | solution.py:23
  314.6 0.0 copy-start
  314.6 0.0 all-gather.12.cloned.1.call-update
  314.6 0.0 all-gather.10.cloned.1.call-start
  314.7 0.5 all-gather.10.cloned.1.call-update
  315.2 0.0 all-gather.14.cloned.1.call-start
  315.3 54.4 %all-gather.12.cloned.1.call-done = bf16[4096,512]{1,0:T(8,128)(2,1)} async-done(((bf16[2048,512]{1,0:T(8,128)(2,1)}), bf16[4096,512]{1,0:T(8,128)(2,1)}) %all-gather.12.cloned.1.call-update) | async-done | bytes 4194320 | tf_op jit(solution)/shard_map/all_gather | solution.py:18
  369.7 3.6 collective-permute-start
  373.3 5.1 collective-permute-done
  378.4 220.5 %all-gather.10.cloned.1.call-done = bf16[2048,4096]{1,0:T(8,128)(2,1)} async-done(((bf16[2048,512]{1,0:T(8,128)(2,1)}), bf16[2048,4096]{1,0:T(8,128)(2,1)}) %all-gather.10.cloned.1.call-update) | async-done | bytes 16777232 | tf_op jit(solution)/shard_map/all_gather | solution.py:22
  598.9 0.0 copy-done
  598.9 14.5 %fusion.18 = bf16[2048,512]{1,0:T(8,128)(2,1)} fusion(bf16[2048,512]{1,0:T(8,128)(2,1)S(1)} %copy-done, bf16[2048,4096]{1,0:T(8,128)(2,1)} %all-gather.10.cloned.1.call-done, bf16[4096,512]{1,0:T(8,128)(2,1)} %collective-permute-done, pred[]{:T(512)S(6)} %ge.3), kind=kOutput, calls=%fused_computation.14 | convolution fusion | flops 8592031744 | bytes 25165824 | tf_op jit(solution)/shard_map/dot_general | solution.py:23
  613.5 0.0 all-gather.14.cloned.1.call-update
  613.5 0.0 all-gather.20.cloned.1.call-start
  613.5 0.5 all-gather.20.cloned.1.call-update
  614.1 54.5 %all-gather.14.cloned.1.call-done = bf16[4096,512]{1,0:T(8,128)(2,1)} async-done(((bf16[2048,512]{1,0:T(8,128)(2,1)}), bf16[4096,512]{1,0:T(8,128)(2,1)}) %all-gather.14.cloned.1.call-update) | async-done | bytes 4194320 | tf_op jit(solution)/shard_map/all_gather | solution.py:18
  668.6 3.6 collective-permute-start.1
  672.2 5.0 collective-permute-done.1
  677.2 15.9 %fusion.14 = bf16[1,2048,512]{2,1,0:T(8,128)(2,1)} fusion(bf16[2048,512]{1,0:T(8,128)(2,1)S(1)} %copy-done, bf16[2048,4096]{1,0:T(8,128)(2,1)} %all-gather.10.cloned.1.call-done, bf16[4096,512]{1,0:T(8,128)(2,1)} %collective-permute-done.1, pred[]{:T(512)S(6)} %gt.4), kind=kOutput, calls=%fused_computation.12 | convolution fusion | flops 8594128896 | bytes 25165824 | tf_op jit(solution)/shard_map/dot_general | solution.py:23
  693.1 0.0 copy-start.1
  693.1 204.6 %all-gather.20.cloned.1.call-done = bf16[1,2048,4096]{2,1,0:T(8,128)(2,1)} async-done(((bf16[1,2048,512]{2,1,0:T(8,128)(2,1)}), bf16[1,2048,4096]{2,1,0:T(8,128)(2,1)}) %all-gather.20.cloned.1.call-update) | async-done | bytes 16777232 | tf_op jit(solution)/shard_map/all_gather | solution.py:22
  897.8 13.9 %fusion.15 = bf16[1,2048,512]{2,1,0:T(8,128)(2,1)S(1)} fusion(bf16[4096,512]{1,0:T(8,128)(2,1)} %collective-permute-done.1, bf16[1,2048,4096]{2,1,0:T(8,128)(2,1)} %all-gather.20.cloned.1.call-done, pred[]{:T(512)S(6)} %gt.4, bf16[2,2048,512]{2,1,0:T(8,128)(2,1)} %param.1), kind=kOutput, calls=%fused_computation.13 | convolution fusion | flops 8594128896 | bytes 25165824 | tf_op jit(solution)/shard_map/dot_general | solution.py:23
  911.7 0.0 copy-done.1
  911.7 2.4 pad_maximum_fusion
Async XLA Ops:
  6.5 64.2 %all-gather.18.cloned.1.call-start = ((), (), s32[]{:S(2)}) async-start(), calls=%async_computation.4 | async-start | bytes 6291456 | tf_op jit(solution)/shard_map/all_gather | solution.py:18
  11.1 289.0 %all-gather.16.cloned.1.call-start = ((), (), s32[]{:S(2)}) async-start(), calls=%async_computation.3 | async-start | bytes 18874368 | tf_op jit(solution)/shard_map/all_gather | solution.py:22
  11.9 357.8 %all-gather.12.cloned.1.call-start = ((), (), s32[]{:S(2)}) async-start(), calls=%async_computation.1 | async-start | bytes 6291456 | tf_op jit(solution)/shard_map/all_gather | solution.py:18
  314.6 284.3 %copy-start = (bf16[2048,512]{1,0:T(8,128)(2,1)S(1)}, bf16[2048,512]{1,0:T(8,128)(2,1)}, u32[]{:S(2)}) copy-start(bf16[2048,512]{1,0:T(8,128)(2,1)} %fusion.9) | copy-start | bytes 6291460
  314.6 284.3 %all-gather.10.cloned.1.call-start = ((), (), s32[]{:S(2)}) async-start(), calls=%async_computation | async-start | bytes 18874368 | tf_op jit(solution)/shard_map/all_gather | solution.py:22
  315.2 353.3 %all-gather.14.cloned.1.call-start = ((), (), s32[]{:S(2)}) async-start(), calls=%async_computation.2 | async-start | bytes 6291456 | tf_op jit(solution)/shard_map/all_gather | solution.py:18
  369.7 8.7 collective-permute-start
  613.5 284.3 %all-gather.20.cloned.1.call-start = ((), (), s32[]{:S(2)}) async-start(), calls=%async_computation.5 | async-start | bytes 18874368 | tf_op jit(solution)/shard_map/all_gather | solution.py:22
  668.6 8.7 collective-permute-start.1
  693.1 218.5 %copy-start.1 = (bf16[1,2048,512]{2,1,0:T(8,128)(2,1)S(1)}, bf16[1,2048,512]{2,1,0:T(8,128)(2,1)}, u32[]{:S(2)}) copy-start(bf16[1,2048,512]{2,1,0:T(8,128)(2,1)} %fusion.14) | copy-start | bytes 6291460
Sparse Core Ops, SparseCore 0:
  11.2 59.4 all-gather.17
  72.8 227.2 all-gather.15
  314.8 54.8 all-gather.11
  371.6 227.2 all-gather.9
  613.6 54.9 all-gather.13
  670.5 227.2 all-gather.19
where the time goes:
time: 921 us
  waiting for transfers between devices  834 us (91%)
  matrix products  58.8 us (6%)
  between operations  13.5 us (1%)
    all_gather x3, waiting for transfers between devices, times_panel(): gathered = lax.all_gather(left_tile, 'row', axis=1, tiled=True)  655 us
    all_gather x3, waiting for transfers between devices, column_panel(): return lax.all_gather(tile, 'seg', axis=0, tiled=True)  168 us
    dot_general x4, matrix products, times_panel(): return jnp.dot(gathered, right_block, preferred_element_type=jnp.float32)  58.8 us
  transfers between devices with their start and end apart: 8, of which 8 were waited for; matrix products, arithmetic and copies ran while one was open for 2% of the time, Pallas kernels for 0%

commit v1 on v0

v1 whole, which is shorter than its diff:
```python
import math

import jax
import jax.numpy as jnp
from jax import lax
from jax.experimental import pallas as pl
from jax.experimental.pallas import tpu as pltpu
from jax.sharding import PartitionSpec as P


def fast_length(mesh):
    count = mesh.shape["row"]
    line = mesh.devices.reshape(mesh.shape["seg"], count, mesh.shape["col"])[0, :, 0]
    coords = [getattr(d, "coords", None) for d in line]
    if count < 2 or any(c is None for c in coords):
        return 1
    moving = [a for a in range(len(coords[0])) if coords[0][a] != coords[1][a]]
    if len(moving) != 1:
        return 1
    length = 1
    while length < count and all(
        coords[length][a] == coords[0][a] for a in range(len(coords[0])) if a != moving[0]
    ):
        length += 1
    return length if count % length == 0 else 1


def after(value, *others):
    return lax.optimization_barrier((value, *others))[0]


def product_kernel(n_left, n_right, by_half, scale, place, *refs):
    left = refs[:n_left]
    right = refs[n_left : n_left + n_right]
    out, lscr, rscr, acc, lsem, rsem = refs[n_left + n_right :]
    _, segs, subs, cores, _, _ = rscr.shape

    def right_target(y, s, c):
        return rscr.at[s, y, :, c] if by_half else rscr.at[:, y, s, c]

    for i in range(n_left):
        k = place[0, i]
        pltpu.make_async_copy(left[i], lscr.at[k], lsem.at[k]).start()
    for i in range(n_right):
        y, s, c = place[1, i], place[2, i], place[3, i]
        pltpu.make_async_copy(right[i], right_target(y, s, c), rsem.at[y, s, c]).start()
    k = 0
    for y in range(segs):
        for s in range(subs):
            for c in range(cores):
                pltpu.make_async_copy(left[0], lscr.at[k], lsem.at[k]).wait()
                for wanted in range(subs) if by_half and s == 0 else ([] if by_half else [s]):
                    pltpu.make_async_copy(right[0], right_target(y, wanted, c), rsem.at[y, wanted, c]).wait()
                for h in range(2):
                    term = jnp.dot(lscr[k], rscr[h, y, s, c], preferred_element_type=jnp.float32)
                    if k == 0:
                        acc[h] = term
                    elif k < segs * subs * cores - 1:
                        acc[h] += term
                    else:
                        out[h] = ((acc[h] + term) * scale).astype(out.dtype)
                k += 1


def product(left, right, by_half, scale, segs, place):
    q, w = left[0].shape
    n_left, n_right = len(left), len(right)

    def body(place_ref, *refs):
        product_kernel(n_left, n_right, by_half, scale, place_ref, *refs)

    order = n_left * w
    return pl.pallas_call(
        body,
        out_shape=jax.ShapeDtypeStruct((2, q, w), jnp.bfloat16),
        in_specs=[pl.BlockSpec(memory_space=pltpu.SMEM)]
        + [pl.BlockSpec(memory_space=pl.ANY)] * (n_left + n_right),
        out_specs=pl.BlockSpec(memory_space=pltpu.VMEM),
        scratch_shapes=[
            pltpu.VMEM((n_left, q, w), jnp.bfloat16),
            pltpu.VMEM((2, segs, 2, 2, q, w), jnp.bfloat16),
            pltpu.VMEM((2, q, w), jnp.float32),
            pltpu.SemaphoreType.DMA((n_left,)),
            pltpu.SemaphoreType.DMA((segs, 2, 2)),
        ],
        cost_estimate=pl.CostEstimate(
            flops=4 * q * order * w, bytes_accessed=2 * order * (q + 2 * w), transcendentals=0
        ),
        compiler_params=pltpu.CompilerParams(vmem_limit_bytes=40 << 20),
    )(place, *left, *right)


def local(fast, slices):
    segs, rows, _ = (lax.axis_size(a) for a in ("seg", "row", "col"))
    slow = rows // fast
    height, w = slices.shape[1:]
    q = height // 4
    y, r, c = (lax.axis_index(a) for a in ("seg", "row", "col"))
    z, x = r // fast, r % fast
    zl = z % 2
    factor = math.sqrt(segs * height)

    def send(value, axes, pairs, gate=None):
        if gate is not None:
            value = after(value, gate)
        return lax.ppermute(value, axes, pairs)

    def along(value, dz, dx, gate=None):
        pairs = [
            (i, ((i // fast + dz) % slow) * fast + (i % fast + dx) % fast) for i in range(rows)
        ]
        return send(value, "row", pairs, gate)

    def seg_shift(value, dy):
        return send(value, "seg", [(i, (i + dy) % segs) for i in range(segs)])

    def partner(i):
        return ((i // fast) ^ 1) * fast + i % fast

    def plane_swap(value, gate=None):
        return send(value, "row", [(i, partner(i)) for i in range(rows)], gate)

    def core_swap(value):
        return send(value, "col", [(0, 1), (1, 0)])

    def row_half(block, i):
        return lax.dynamic_index_in_dim(block, i, 0, keepdims=False)

    class Left:
        def __init__(self, block):
            self.same, self.other = row_half(block, zl), row_half(block, 1 - zl)
            self.pieces = []

        def over_slow(self, j, gate=None):
            piece = along(self.same if j % 2 == 0 else self.other, j, 0, gate)
            return j, piece

        def over_fast(self, j_piece):
            j, piece = j_piece
            self.pieces.append((j, 0, piece))
            for i in range(1, fast):
                self.pieces.append((j, i, along(piece, 0, i)))

        def places(self):
            return [((z - j) % slow) * fast + (x - i) % fast for j, i, _ in self.pieces]

    class Right:
        def __init__(self, block):
            self.pieces = [(0, 0, 0, block)]

        def places(self):
            return [
                [(y - dy) % segs for dy, _, _, _ in self.pieces],
                [zl ^ s for _, s, _, _ in self.pieces],
                [c ^ k for _, _, k, _ in self.pieces],
            ]

        def near(self, gate=None):
            block = self.pieces[0][-1]
            self.plane = plane_swap(block, gate)
            self.pieces.append((0, 1, 0, self.plane))
            for dy in range(1, segs):
                self.pieces.append((dy, 0, 0, seg_shift(block, dy)))

        def far(self):
            for dy in range(1, segs):
                self.pieces.append((dy, 1, 0, seg_shift(self.plane, dy)))

        def cross(self, dy, s):
            (block,) = [b for p, t, k, b in self.pieces if (p, t, k) == (dy, s, 0)]
            self.pieces.append((dy, s, 1, core_swap(block)))

    def multiply(left, right, by_half, scale):
        table = [left.places()] + right.places()
        width = max(len(t) for t in table)
        zero = jnp.int32(0)
        place = jnp.stack(
            [jnp.stack([jnp.asarray(v, jnp.int32) for v in t] + [zero] * (width - len(t))) for t in table]
        )
        return product(
            [p[-1] for p in left.pieces], [p[-1] for p in right.pieces], by_half, scale, segs, place
        )

    def own_block(right):
        found = {(s, k): row_half(b, zl) for dy, s, k, b in right.pieces if dy == 0}

        def pick(s, k):
            by_core = [jnp.where(c == k, found[(t, 0)], found[(t, 1)]) for t in range(2)]
            return jnp.where(zl == s, by_core[0], by_core[1])

        return jnp.stack([jnp.stack([pick(s, k) for k in range(2)]) for s in range(2)])

    parts = slices.reshape(2, 2, 2, q, w)
    mine = lax.dynamic_index_in_dim(parts, c, 2, keepdims=False)
    theirs = core_swap(lax.dynamic_index_in_dim(parts, 1 - c, 2, keepdims=False))
    right = Right(jnp.where(c == 0, mine[0], theirs[0]))
    lefts = [
        Left(jnp.where(c == 0, mine[1], theirs[1])),
        Left(jnp.where(c == 0, theirs[0], mine[0])),
        Left(jnp.where(c == 0, theirs[1], mine[1])),
    ]
    evens, odds = range(2, slow, 2), range(1, slow, 2)

    left = lefts[0]
    right.near()
    pending = [left.over_slow(j) for j in evens]
    for item in lefts:
        item.over_fast((0, item.same))
    right.cross(0, 0)
    for item in pending:
        left.over_fast(item)
    gate, before = right.plane, None
    for j in odds:
        item = left.over_slow(j, gate)
        if before is None:
            right.far()
            right.cross(0, 1)
            for dy in range(1, segs):
                right.cross(dy, 0)
        else:
            left.over_fast(before)
        gate, before = item[1], item

    rights = []
    for n in range(3):
        following = lefts[n + 1] if n < 2 else None
        if following:
            early = [following.over_slow(j, gate) for j in (*evens, *odds[:1])]
        left.over_fast(before)
        for dy in range(1, segs):
            right.cross(dy, 1)
        carried = multiply(left, right, n == 0, factor if n == 2 else 1.0)
        rights.append(right)
        if not following:
            break
        left, right = following, Right(carried)
        right.near()
        right.cross(0, 0)
        for item in early:
            left.over_fast(item)
        gate, before = right.plane, None
        right.far()
        for j in odds[1:]:
            item = left.over_slow(j, gate)
            if before is None:
                right.cross(0, 1)
                for dy in range(1, segs):
                    right.cross(dy, 0)
            else:
                left.over_fast(before)
            gate, before = item[1], item

    keep, away = row_half(carried, zl), row_half(carried, 1 - zl)
    moved = [
        send(away, ("row", "col"), [(i * 2 + k, partner(i) * 2 + 1) for i in range(rows)])
        for k in range(2)
    ]
    kept = send(keep, "col", [(0, 1)])
    local_rows = jnp.stack([kept, keep])
    far_rows = jnp.stack(moved)
    final = jnp.stack([jnp.where(zl == s, local_rows, far_rows) for s in range(2)])

    def scaled(value):
        return (value.astype(jnp.float32) * factor).astype(jnp.bfloat16)

    head = jnp.where(c == 0, slices[0].reshape(2, 2, q, w), own_block(rights[2]))
    tail = jnp.where(c == 0, scaled(own_block(rights[1])), final)
    return jnp.stack([scaled(head).reshape(height, w), tail.reshape(height, w)], axis=0)


def solution(mesh):
    spec = P("col", "seg", "row")
    fast = fast_length(mesh)

    def body(slices):
        return local(fast, slices)

    return jax.shard_map(body, mesh=mesh, in_specs=(spec,), out_specs=spec, check_vma=False)
```

time: 921 us -> 330 us (0.36)
  waiting for transfers between devices: 834 us -> 223 us
  matrix products: 58.8 us -> 0 us
  starting transfers between devices: 7.42 us -> 56.7 us
  Pallas kernels: 0 us -> 23.2 us
  between operations: 13.5 us -> 0.27 us
    all_gather x6 -> x0, waiting for transfers between devices: 822 us -> none  [the longest x3 655 us: times_panel(): gathered = lax.all_gather(left_tile, 'row', axis=1, tiled=True)]
    ppermute x2 -> x46, waiting for transfers between devices: 10.1 us -> 223 us  [send(): return lax.ppermute(value, axes, pairs)]
    dot_general x4 -> x0, matrix products: 58.8 us -> none  [times_panel(): return jnp.dot(gathered, right_block, preferred_element_type=jnp.float32)]
    ppermute x2 -> x46, starting transfers between devices: 7.22 us -> 56.7 us  [send(): return lax.ppermute(value, axes, pairs)]
    pallas_call x0 -> x3, Pallas kernels: none -> 23.2 us  [product(): pl.pallas_call(body, out_shape=jax.ShapeDtypeStruct((2, q, w), jnp.bfloat...]
  transfers between devices with their start and end apart: 8 -> 46, of which waited for: 8 -> 23; matrix products, arithmetic and copies ran while one was open for 2% -> 2% of each run, Pallas kernels for 0% -> 0%
where the time goes in v1:
time: 330 us; the launch traced here: 328 us
  waiting for transfers between devices  223 us (68%)
  starting transfers between devices  56.7 us (17%)
  Pallas kernels  23.2 us (7%)
  local copies, waits for them, and re-layouts  13.4 us (4%)
  other arithmetic  11.5 us (3%)
    ppermute x46, waiting for transfers between devices, send(): return lax.ppermute(value, axes, pairs)  223 us
    ppermute x46, starting transfers between devices, send(): return lax.ppermute(value, axes, pairs)  56.7 us
    pallas_call x3, Pallas kernels, product(): pl.pallas_call(body, out_shape=jax.ShapeDtypeStruct((2, q, w), jnp.bfloat...  23.2 us
    unnamed x30, local copies, waits for them, and re-layouts  9.01 us
  transfers between devices with their start and end apart: 46, of which 23 were waited for; matrix products, arithmetic and copies ran while one was open for 2% of the time, Pallas kernels for 0%

profile of v1, /device:TPU:0, one launch (start us, length us, event | category | flops | bytes accessed | tf_op | source)
XLA Modules:
  0.0 328.5 jit_solution(11715028842495117521)
XLA Ops:
  2.3 3.9 %collective-permute-done = bf16[2,2,512,512]{3,2,1,0:T(8,128)(2,1)} collective-permute-done((bf16[2,2,512,512]{3,2,1,0:T(8,128)(2,1)S(1)}, bf16[2,2,512,512]{3,2,1,0:T(8,128)(2,1)}, u32[]{:S(2)}, u32[]{:S(2)}) %collective-permute-start) | collective-permute-done | bytes 2097184 | tf_op jit(solution)/shard_map/ppermute | solution.py:106
  6.2 4.0 %broadcast_select_fusion.5 = (bf16[2,512,512]{2,1,0:T(8,128)(2,1)}, bf16[2,512,512]{2,1,0:T(8,128)(2,1)}, bf16[2,512,512]{2,1,0:T(8,128)(2,1)S(1)}, bf16[2,512,512]{2,1,0:T(8,128)(2,1)}) fusion(pred[]{:T(512)S(6)} %eq.115, bf16[2,2,512,512]{3,2,1,0:T(8,128)(2,1)} %collective-permute-done, bf16[2,2,2,512,512]{4,3,2,1,0:T(8,128)(2,1)} %bitcast.82, ...), kind=kLoop, calls=%fused_computation.21 | loop fusion | flops 2097152 | bytes 8388617 | tf_op jit(solution)/shard_map/jit(_where)/select_n | solution.py:199
  10.2 2.9 collective-permute-start.2
  15.9 2.7 collective-permute-start.10
  18.6 29.2 %collective-permute-done.2.refs_9_ = bf16[2,512,512]{2,1,0:T(8,128)(2,1)S(1)} collective-permute-done((bf16[2,512,512]{2,1,0:T(8,128)(2,1)S(1)}, bf16[2,512,512]{2,1,0:T(8,128)(2,1)S(1)}, u32[]{:S(2)}, u32[]{:S(2)}) %collective-permute-start.2) | collective-permute-done | bytes 1048608 | tf_op jit(solution)/shard_map/ppermute | solution.py:106
  51.5 12.8 %collective-permute-done.3.refs_4_ = bf16[512,512]{1,0:T(8,128)(2,1)} collective-permute-done((bf16[512,512]{1,0:T(8,128)(2,1)S(1)}, bf16[512,512]{1,0:T(8,128)(2,1)}, u32[]{:S(2)}, u32[]{:S(2)}) %collective-permute-start.3) | collective-permute-done | bytes 524320 | tf_op jit(solution)/shard_map/ppermute | solution.py:106
  65.1 3.8 %collective-permute-start.4 = (bf16[512,512]{1,0:T(8,128)(2,1)S(1)}, bf16[512,512]{1,0:T(8,128)(2,1)}, u32[]{:S(2)}, u32[]{:S(2)}) collective-permute-start(bf16[512,512]{1,0:T(8,128)(2,1)S(1)} %get-tuple-element.14), channel_id=1, source_target_pairs={{0,12},{2,14},{4,0},{6,2},{8,4},{10,6},{12,8},{14,10},{1,13},{3,15... | collective-permute-start | bytes 1572872 | tf_op jit(solution)/shard_map/ppermute | solution.py:106
  75.9 3.6 %collective-permute-done.4.refs_6_ = bf16[512,512]{1,0:T(8,128)(2,1)} collective-permute-done((bf16[512,512]{1,0:T(8,128)(2,1)S(1)}, bf16[512,512]{1,0:T(8,128)(2,1)}, u32[]{:S(2)}, u32[]{:S(2)}) %collective-permute-start.4) | collective-permute-done | bytes 524320 | tf_op jit(solution)/shard_map/ppermute | solution.py:106
  81.4 8.1 %collective-permute-done.12.refs_5_ = bf16[512,512]{1,0:T(8,128)(2,1)} collective-permute-done((bf16[512,512]{1,0:T(8,128)(2,1)}, bf16[512,512]{1,0:T(8,128)(2,1)}, u32[]{:S(2)}, u32[]{:S(2)}) %collective-permute-start.12) | collective-permute-done | bytes 524320 | tf_op jit(solution)/shard_map/ppermute | solution.py:106
  89.5 9.7 %collective-permute-done.13.refs_7_ = bf16[512,512]{1,0:T(8,128)(2,1)} collective-permute-done((bf16[512,512]{1,0:T(8,128)(2,1)}, bf16[512,512]{1,0:T(8,128)(2,1)}, u32[]{:S(2)}, u32[]{:S(2)}) %collective-permute-start.13) | collective-permute-done | bytes 524320 | tf_op jit(solution)/shard_map/ppermute | solution.py:106
  103.8 7.7 %shard_map.17.refs_8_ = bf16[2,512,512]{2,1,0:T(8,128)(2,1)S(1)} custom-call(s32[4,8]{1,0:T(4,128)S(1)} %pad_add_fusion.place_ref, bf16[512,512]{1,0:T(8,128)(2,1)S(1)} %get-tuple-element.43.refs_0_, bf16[512,512]{1,0:T(8,128)(2,1)S(1)} %copy-done.7, bf16[512,512]{1,0:T(8,128)(2,1)S(1)} %collective-permute-done.10.refs_2_, bf16[512,512]{1,0:T(8,128)(2,1)S(1)} %copy-done.9, ...), custom_call_target="tpu_custom_call" | custom-call | flops 4294967296 | bytes 12582912 | tf_op jit(solution)/shard_map/pallas_call | solution.py:73
  112.1 3.7 %collective-permute-start.5 = (bf16[512,512]{1,0:T(8,128)(2,1)S(1)}, bf16[512,512]{1,0:T(8,128)(2,1)S(1)}, u32[]{:S(2)}, u32[]{:S(2)}) collective-permute-start(bf16[512,512]{1,0:T(8,128)(2,1)S(1)} %get-tuple-element.15.refs_0_), channel_id=1, source_target_pairs={{0,8},{2,10},{4,12},{6,14},{8,0},{10,2},{12,4},{14,6},{1,9},{3,11}... | collective-permute-start | bytes 1572872 | tf_op jit(solution)/shard_map/ppermute | solution.py:106
  117.9 29.4 %collective-permute-done.20.refs_9_ = bf16[2,512,512]{2,1,0:T(8,128)(2,1)S(1)} collective-permute-done((bf16[2,512,512]{2,1,0:T(8,128)(2,1)S(1)}, bf16[2,512,512]{2,1,0:T(8,128)(2,1)S(1)}, u32[]{:S(2)}, u32[]{:S(2)}) %collective-permute-start.20) | collective-permute-done | bytes 1048608 | tf_op jit(solution)/shard_map/ppermute | solution.py:106
  147.3 2.5 collective-permute-start.25
  151.9 8.0 %collective-permute-done.7.refs_4_ = bf16[512,512]{1,0:T(8,128)(2,1)S(1)} collective-permute-done((bf16[512,512]{1,0:T(8,128)(2,1)S(1)}, bf16[512,512]{1,0:T(8,128)(2,1)S(1)}, u32[]{:S(2)}, u32[]{:S(2)}) %collective-permute-start.7) | collective-permute-done | bytes 524320 | tf_op jit(solution)/shard_map/ppermute | solution.py:106
  161.4 3.2 collective-permute-done.1.refs_1_
  164.7 11.2 %collective-permute-done.6.refs_3_ = bf16[512,512]{1,0:T(8,128)(2,1)S(1)} collective-permute-done((bf16[512,512]{1,0:T(8,128)(2,1)S(1)}, bf16[512,512]{1,0:T(8,128)(2,1)S(1)}, u32[]{:S(2)}, u32[]{:S(2)}) %collective-permute-start.6) | collective-permute-done | bytes 524320 | tf_op jit(solution)/shard_map/ppermute | solution.py:106
  175.9 4.6 %collective-permute-start.21 = (bf16[512,512]{1,0:T(8,128)(2,1)S(1)}, bf16[512,512]{1,0:T(8,128)(2,1)S(1)}, u32[]{:S(2)}, u32[]{:S(2)}) collective-permute-start(bf16[512,512]{1,0:T(8,128)(2,1)S(1)} %get-tuple-element.16), channel_id=1, source_target_pairs={{0,12},{2,14},{4,0},{6,2},{8,4},{10,6},{12,8},{14,10},{1,13},{3,15... | collective-permute-start | bytes 1572872 | tf_op jit(solution)/shard_map/ppermute | solution.py:106
  180.5 4.6 %collective-permute-done.8.refs_5_ = bf16[512,512]{1,0:T(8,128)(2,1)S(1)} collective-permute-done((bf16[512,512]{1,0:T(8,128)(2,1)S(1)}, bf16[512,512]{1,0:T(8,128)(2,1)S(1)}, u32[]{:S(2)}, u32[]{:S(2)}) %collective-permute-start.8) | collective-permute-done | bytes 524320 | tf_op jit(solution)/shard_map/ppermute | solution.py:106
  188.7 10.8 %collective-permute-done.22.refs_7_ = bf16[512,512]{1,0:T(8,128)(2,1)S(1)} collective-permute-done((bf16[512,512]{1,0:T(8,128)(2,1)S(1)}, bf16[512,512]{1,0:T(8,128)(2,1)S(1)}, u32[]{:S(2)}, u32[]{:S(2)}) %collective-permute-start.22) | collective-permute-done | bytes 524320 | tf_op jit(solution)/shard_map/ppermute | solution.py:106
  199.5 7.6 %shard_map.18.refs_8_ = bf16[2,512,512]{2,1,0:T(8,128)(2,1)} custom-call(s32[4,8]{1,0:T(4,128)S(1)} %pad_add_fusion.place_ref, bf16[512,512]{1,0:T(8,128)(2,1)S(1)} %get-tuple-element.15.refs_0_, bf16[512,512]{1,0:T(8,128)(2,1)S(1)} %collective-permute-done.1.refs_1_, bf16[512,512]{1,0:T(8,128)(2,1)S(1)} %collective-permute-done.5.refs_2_, ...), custom_call_target="tpu_custom_call" | custom-call | flops 4294967296 | bytes 12582912 | tf_op jit(solution)/shard_map/pallas_call | solution.py:73
  209.7 4.1 %collective-permute-start.33 = (bf16[512,512]{1,0:T(8,128)(2,1)S(1)}, bf16[512,512]{1,0:T(8,128)(2,1)S(1)}, u32[]{:S(2)}, u32[]{:S(2)}) collective-permute-start(bf16[512,512]{1,0:T(8,128)(2,1)S(1)} %get-tuple-element.18.refs_0_), channel_id=1, source_target_pairs={{0,8},{2,10},{4,12},{6,14},{8,0},{10,2},{12,4},{14,6},{1,9},{3,11}... | collective-permute-start | bytes 1572872 | tf_op jit(solution)/shard_map/ppermute | solution.py:106
  214.1 27.2 %collective-permute-done.30.refs_9_ = bf16[2,512,512]{2,1,0:T(8,128)(2,1)} collective-permute-done((bf16[2,512,512]{2,1,0:T(8,128)(2,1)}, bf16[2,512,512]{2,1,0:T(8,128)(2,1)}, u32[]{:S(2)}, u32[]{:S(2)}) %collective-permute-start.30) | collective-permute-done | bytes 1048608 | tf_op jit(solution)/shard_map/ppermute | solution.py:106
  243.2 13.4 %collective-permute-done.35.refs_4_ = bf16[512,512]{1,0:T(8,128)(2,1)} collective-permute-done((bf16[512,512]{1,0:T(8,128)(2,1)}, bf16[512,512]{1,0:T(8,128)(2,1)}, u32[]{:S(2)}, u32[]{:S(2)}) %collective-permute-start.35) | collective-permute-done | bytes 524320 | tf_op jit(solution)/shard_map/ppermute | solution.py:106
  256.7 6.8 %collective-permute-done.40.refs_12_ = bf16[2,512,512]{2,1,0:T(8,128)(2,1)} collective-permute-done((bf16[2,512,512]{2,1,0:T(8,128)(2,1)}, bf16[2,512,512]{2,1,0:T(8,128)(2,1)}, u32[]{:S(2)}, u32[]{:S(2)}) %collective-permute-start.40) | collective-permute-done | bytes 1048608 | tf_op jit(solution)/shard_map/ppermute | solution.py:106
  264.9 3.1 collective-permute-start.34
  272.4 8.5 %collective-permute-done.34.refs_3_ = bf16[512,512]{1,0:T(8,128)(2,1)S(1)} collective-permute-done((bf16[512,512]{1,0:T(8,128)(2,1)S(1)}, bf16[512,512]{1,0:T(8,128)(2,1)S(1)}, u32[]{:S(2)}, u32[]{:S(2)}) %collective-permute-start.34) | collective-permute-done | bytes 524320 | tf_op jit(solution)/shard_map/ppermute | solution.py:106
  280.9 11.2 %collective-permute-done.36.refs_5_ = bf16[512,512]{1,0:T(8,128)(2,1)S(1)} collective-permute-done((bf16[512,512]{1,0:T(8,128)(2,1)}, bf16[512,512]{1,0:T(8,128)(2,1)S(1)}, u32[]{:S(2)}, u32[]{:S(2)}) %collective-permute-start.36) | collective-permute-done | bytes 524320 | tf_op jit(solution)/shard_map/ppermute | solution.py:106
  292.1 11.1 %collective-permute-done.38.refs_7_ = bf16[512,512]{1,0:T(8,128)(2,1)S(1)} collective-permute-done((bf16[512,512]{1,0:T(8,128)(2,1)}, bf16[512,512]{1,0:T(8,128)(2,1)S(1)}, u32[]{:S(2)}, u32[]{:S(2)}) %collective-permute-start.38) | collective-permute-done | bytes 524320 | tf_op jit(solution)/shard_map/ppermute | solution.py:106
  303.2 8.0 %shard_map.19 = bf16[2,512,512]{2,1,0:T(8,128)(2,1)S(1)} custom-call(s32[4,8]{1,0:T(4,128)S(1)} %pad_add_fusion.place_ref, bf16[512,512]{1,0:T(8,128)(2,1)S(1)} %get-tuple-element.18.refs_0_, bf16[512,512]{1,0:T(8,128)(2,1)S(1)} %collective-permute-done.32.refs_1_, bf16[512,512]{1,0:T(8,128)(2,1)S(1)} %copy-done.11, ...), custom_call_target="tpu_custom_call" | custom-call | flops 4294967296 | bytes 12582912 | tf_op jit(solution)/shard_map/pallas_call | solution.py:73
  312.0 5.0 %collective-permute-start.44 = (bf16[512,512]{1,0:T(8,128)(2,1)S(1)}, bf16[512,512]{1,0:T(8,128)(2,1)S(1)}, u32[]{:S(2)}, u32[]{:S(2)}) collective-permute-start(bf16[512,512]{1,0:T(8,128)(2,1)S(1)} %get-tuple-element.37), channel_id=1, source_target_pairs={{0,5},{2,7},{4,1},{6,3},{8,13},{10,15},{12,9},{14,11},{16,21},{18,... | collective-permute-start | bytes 1572872 | tf_op jit(solution)/shard_map/ppermute | solution.py:106
  319.9 5.5 %collective-permute-done.44 = bf16[512,512]{1,0:T(8,128)(2,1)S(1)} collective-permute-done((bf16[512,512]{1,0:T(8,128)(2,1)S(1)}, bf16[512,512]{1,0:T(8,128)(2,1)S(1)}, u32[]{:S(2)}, u32[]{:S(2)}) %collective-permute-start.44) | collective-permute-done | bytes 524320 | tf_op jit(solution)/shard_map/ppermute | solution.py:106
  (113 shorter events, 50.1 us)
Async XLA Ops:
  10.2 37.6 %collective-permute-start.2 = (bf16[2,512,512]{2,1,0:T(8,128)(2,1)S(1)}, bf16[2,512,512]{2,1,0:T(8,128)(2,1)S(1)}, u32[]{:S(2)}, u32[]{:S(2)}) collective-permute-start(bf16[2,512,512]{2,1,0:T(8,128)(2,1)S(1)} %get-tuple-element.23.refs_8_), channel_id=1, source_target_pairs={{0,4},{2,6},{4,0},{6,2},{8,12},{10,14},{12,8},{14,10},{1,5},{3,7},... | collective-permute-start | bytes 3145736 | tf_op jit(solution)/shard_map/ppermute | solution.py:106
  13.1 37.9 %collective-permute-start.14 = (bf16[2,512,512]{2,1,0:T(8,128)(2,1)S(1)}, bf16[2,512,512]{2,1,0:T(8,128)(2,1)}, u32[]{:S(2)}, u32[]{:S(2)}) collective-permute-start(bf16[2,512,512]{2,1,0:T(8,128)(2,1)S(1)} %get-tuple-element.23.refs_8_), channel_id=1, source_target_pairs={{0,16},{16,0},{1,17},{17,1},{2,18},{18,2},{3,19},{19,3},{4,20},{20... | collective-permute-start | bytes 3145736 | tf_op jit(solution)/shard_map/ppermute | solution.py:106
  15.9 33.6 %collective-permute-start.10 = (bf16[512,512]{1,0:T(8,128)(2,1)S(1)}, bf16[512,512]{1,0:T(8,128)(2,1)S(1)}, u32[]{:S(2)}, u32[]{:S(2)}) collective-permute-start(bf16[512,512]{1,0:T(8,128)(2,1)S(1)} %get-tuple-element.43.refs_0_), channel_id=1, source_target_pairs={{0,8},{2,10},{4,12},{6,14},{8,0},{10,2},{12,4},{14,6},{1,9},{3,11}... | collective-permute-start | bytes 1572872 | tf_op jit(solution)/shard_map/ppermute | solution.py:106
  18.6 50.3 %collective-permute-start.15 = (bf16[2,512,512]{2,1,0:T(8,128)(2,1)S(1)}, bf16[2,512,512]{2,1,0:T(8,128)(2,1)S(1)}, u32[]{:S(2)}, u32[]{:S(2)}) collective-permute-start(bf16[2,512,512]{2,1,0:T(8,128)(2,1)S(1)} %get-tuple-element.23.refs_8_), channel_id=1, source_target_pairs={{0,1},{1,0},{2,3},{3,2},{4,5},{5,4},{6,7},{7,6},{8,9},{9,8},{10,11... | collective-permute-start | bytes 3145736 | tf_op jit(solution)/shard_map/ppermute | solution.py:106
  47.8 24.7 %collective-permute-start.16 = (bf16[2,512,512]{2,1,0:T(8,128)(2,1)S(1)}, bf16[2,512,512]{2,1,0:T(8,128)(2,1)}, u32[]{:S(2)}, u32[]{:S(2)}) collective-permute-start(bf16[2,512,512]{2,1,0:T(8,128)(2,1)S(1)} %collective-permute-done.2.refs_9_), channel_id=1, source_target_pairs={{0,16},{16,0},{1,17},{17,1},{2,18},{18,2},{3,19},{19,3},{4,20},{20... | collective-permute-start | bytes 3145736 | tf_op jit(solution)/shard_map/ppermute | solution.py:106
  49.5 14.8 %collective-permute-start.9 = (bf16[512,512]{1,0:T(8,128)(2,1)S(1)}, bf16[512,512]{1,0:T(8,128)(2,1)S(1)}, u32[]{:S(2)}, u32[]{:S(2)}) collective-permute-start(bf16[512,512]{1,0:T(8,128)(2,1)S(1)} %get-tuple-element.43.refs_0_), channel_id=1, source_target_pairs={{0,2},{2,0},{4,6},{6,4},{8,10},{10,8},{12,14},{14,12},{1,3},{3,1},... | collective-permute-start | bytes 1572872 | tf_op jit(solution)/shard_map/ppermute | solution.py:106
  51.0 22.6 %collective-permute-start.11 = (bf16[512,512]{1,0:T(8,128)(2,1)S(1)}, bf16[512,512]{1,0:T(8,128)(2,1)S(1)}, u32[]{:S(2)}, u32[]{:S(2)}) collective-permute-start(bf16[512,512]{1,0:T(8,128)(2,1)S(1)} %collective-permute-done.10.refs_2_), channel_id=1, source_target_pairs={{0,2},{2,0},{4,6},{6,4},{8,10},{10,8},{12,14},{14,12},{1,3},{3,1},... | collective-permute-start | bytes 1572872 | tf_op jit(solution)/shard_map/ppermute | solution.py:106
  64.3 25.2 %collective-permute-start.18 = (bf16[2,512,512]{2,1,0:T(8,128)(2,1)}, bf16[2,512,512]{2,1,0:T(8,128)(2,1)}, u32[]{:S(2)}, u32[]{:S(2)}) collective-permute-start(bf16[2,512,512]{2,1,0:T(8,128)(2,1)} %collective-permute-done.14.refs_10_), channel_id=1, source_target_pairs={{0,1},{1,0},{2,3},{3,2},{4,5},{5,4},{6,7},{7,6},{8,9},{9,8},{10,11... | collective-permute-start | bytes 3145736 | tf_op jit(solution)/shard_map/ppermute | solution.py:106
  69.9 19.6 %collective-permute-start.17 = (bf16[2,512,512]{2,1,0:T(8,128)(2,1)S(1)}, bf16[2,512,512]{2,1,0:T(8,128)(2,1)}, u32[]{:S(2)}, u32[]{:S(2)}) collective-permute-start(bf16[2,512,512]{2,1,0:T(8,128)(2,1)S(1)} %collective-permute-done.2.refs_9_), channel_id=1, source_target_pairs={{0,1},{1,0},{2,3},{3,2},{4,5},{5,4},{6,7},{7,6},{8,9},{9,8},{10,11... | collective-permute-start | bytes 3145736 | tf_op jit(solution)/shard_map/ppermute | solution.py:106
  72.5 26.7 %collective-permute-start.19 = (bf16[2,512,512]{2,1,0:T(8,128)(2,1)}, bf16[2,512,512]{2,1,0:T(8,128)(2,1)}, u32[]{:S(2)}, u32[]{:S(2)}) collective-permute-start(bf16[2,512,512]{2,1,0:T(8,128)(2,1)} %collective-permute-done.16.refs_12_), channel_id=1, source_target_pairs={{0,1},{1,0},{2,3},{3,2},{4,5},{5,4},{6,7},{7,6},{8,9},{9,8},{10,11... | collective-permute-start | bytes 3145736 | tf_op jit(solution)/shard_map/ppermute | solution.py:106
  74.4 15.1 %collective-permute-start.12 = (bf16[512,512]{1,0:T(8,128)(2,1)}, bf16[512,512]{1,0:T(8,128)(2,1)}, u32[]{:S(2)}, u32[]{:S(2)}) collective-permute-start(bf16[512,512]{1,0:T(8,128)(2,1)} %collective-permute-done.3.refs_4_), channel_id=1, source_target_pairs={{0,2},{2,0},{4,6},{6,4},{8,10},{10,8},{12,14},{14,12},{1,3},{3,1},... | collective-permute-start | bytes 1572872 | tf_op jit(solution)/shard_map/ppermute | solution.py:106
  79.5 19.7 %collective-permute-start.13 = (bf16[512,512]{1,0:T(8,128)(2,1)}, bf16[512,512]{1,0:T(8,128)(2,1)}, u32[]{:S(2)}, u32[]{:S(2)}) collective-permute-start(bf16[512,512]{1,0:T(8,128)(2,1)} %collective-permute-done.4.refs_6_), channel_id=1, source_target_pairs={{0,2},{2,0},{4,6},{6,4},{8,10},{10,8},{12,14},{14,12},{1,3},{3,1},... | collective-permute-start | bytes 1572872 | tf_op jit(solution)/shard_map/ppermute | solution.py:106
  111.5 35.9 %collective-permute-start.20 = (bf16[2,512,512]{2,1,0:T(8,128)(2,1)S(1)}, bf16[2,512,512]{2,1,0:T(8,128)(2,1)S(1)}, u32[]{:S(2)}, u32[]{:S(2)}) collective-permute-start(bf16[2,512,512]{2,1,0:T(8,128)(2,1)S(1)} %shard_map.17.refs_8_), channel_id=1, source_target_pairs={{0,4},{2,6},{4,0},{6,2},{8,12},{10,14},{12,8},{14,10},{1,5},{3,7},... | collective-permute-start | bytes 3145736 | tf_op jit(solution)/shard_map/ppermute | solution.py:106
  112.1 39.4 %collective-permute-start.5 = (bf16[512,512]{1,0:T(8,128)(2,1)S(1)}, bf16[512,512]{1,0:T(8,128)(2,1)S(1)}, u32[]{:S(2)}, u32[]{:S(2)}) collective-permute-start(bf16[512,512]{1,0:T(8,128)(2,1)S(1)} %get-tuple-element.15.refs_0_), channel_id=1, source_target_pairs={{0,8},{2,10},{4,12},{6,14},{8,0},{10,2},{12,4},{14,6},{1,9},{3,11}... | collective-permute-start | bytes 1572872 | tf_op jit(solution)/shard_map/ppermute | solution.py:106
  115.7 64.7 %collective-permute-start.23 = (bf16[2,512,512]{2,1,0:T(8,128)(2,1)S(1)}, bf16[2,512,512]{2,1,0:T(8,128)(2,1)S(1)}, u32[]{:S(2)}, u32[]{:S(2)}) collective-permute-start(bf16[2,512,512]{2,1,0:T(8,128)(2,1)S(1)} %shard_map.17.refs_8_), channel_id=1, source_target_pairs={{0,16},{16,0},{1,17},{17,1},{2,18},{18,2},{3,19},{19,3},{4,20},{20... | collective-permute-start | bytes 3145736 | tf_op jit(solution)/shard_map/ppermute | solution.py:106
  117.9 42.1 %collective-permute-start.7 = (bf16[512,512]{1,0:T(8,128)(2,1)S(1)}, bf16[512,512]{1,0:T(8,128)(2,1)S(1)}, u32[]{:S(2)}, u32[]{:S(2)}) collective-permute-start(bf16[512,512]{1,0:T(8,128)(2,1)S(1)} %get-tuple-element.16), channel_id=1, source_target_pairs={{0,4},{2,6},{4,8},{6,10},{8,12},{10,14},{12,0},{14,2},{1,5},{3,7},... | collective-permute-start | bytes 1572872 | tf_op jit(solution)/shard_map/ppermute | solution.py:106
  147.3 37.7 %collective-permute-start.25 = (bf16[2,512,512]{2,1,0:T(8,128)(2,1)S(1)}, bf16[2,512,512]{2,1,0:T(8,128)(2,1)S(1)}, u32[]{:S(2)}, u32[]{:S(2)}) collective-permute-start(bf16[2,512,512]{2,1,0:T(8,128)(2,1)S(1)} %collective-permute-done.20.refs_9_), channel_id=1, source_target_pairs={{0,16},{16,0},{1,17},{17,1},{2,18},{18,2},{3,19},{19,3},{4,20},{20... | collective-permute-start | bytes 3145736 | tf_op jit(solution)/shard_map/ppermute | solution.py:106
  151.5 24.4 %collective-permute-start.6 = (bf16[512,512]{1,0:T(8,128)(2,1)S(1)}, bf16[512,512]{1,0:T(8,128)(2,1)S(1)}, u32[]{:S(2)}, u32[]{:S(2)}) collective-permute-start(bf16[512,512]{1,0:T(8,128)(2,1)S(1)} %collective-permute-done.5.refs_2_), channel_id=1, source_target_pairs={{0,2},{2,0},{4,6},{6,4},{8,10},{10,8},{12,14},{14,12},{1,3},{3,1},... | collective-permute-start | bytes 1572872 | tf_op jit(solution)/shard_map/ppermute | solution.py:106
  159.9 25.1 %collective-permute-start.8 = (bf16[512,512]{1,0:T(8,128)(2,1)S(1)}, bf16[512,512]{1,0:T(8,128)(2,1)S(1)}, u32[]{:S(2)}, u32[]{:S(2)}) collective-permute-start(bf16[512,512]{1,0:T(8,128)(2,1)S(1)} %collective-permute-done.7.refs_4_), channel_id=1, source_target_pairs={{0,2},{2,0},{4,6},{6,4},{8,10},{10,8},{12,14},{14,12},{1,3},{3,1},... | collective-permute-start | bytes 1572872 | tf_op jit(solution)/shard_map/ppermute | solution.py:106
  164.7 24.0 %collective-permute-start.24 = (bf16[2,512,512]{2,1,0:T(8,128)(2,1)S(1)}, bf16[2,512,512]{2,1,0:T(8,128)(2,1)S(1)}, u32[]{:S(2)}, u32[]{:S(2)}) collective-permute-start(bf16[2,512,512]{2,1,0:T(8,128)(2,1)S(1)} %shard_map.17.refs_8_), channel_id=1, source_target_pairs={{0,1},{1,0},{2,3},{3,2},{4,5},{5,4},{6,7},{7,6},{8,9},{9,8},{10,11... | collective-permute-start | bytes 3145736 | tf_op jit(solution)/shard_map/ppermute | solution.py:106
  207.1 34.3 %collective-permute-start.30 = (bf16[2,512,512]{2,1,0:T(8,128)(2,1)}, bf16[2,512,512]{2,1,0:T(8,128)(2,1)}, u32[]{:S(2)}, u32[]{:S(2)}) collective-permute-start(bf16[2,512,512]{2,1,0:T(8,128)(2,1)} %shard_map.18.refs_8_), channel_id=1, source_target_pairs={{0,4},{2,6},{4,0},{6,2},{8,12},{10,14},{12,8},{14,10},{1,5},{3,7},... | collective-permute-start | bytes 3145736 | tf_op jit(solution)/shard_map/ppermute | solution.py:106
  208.0 33.9 %collective-permute-start.32 = (bf16[512,512]{1,0:T(8,128)(2,1)S(1)}, bf16[512,512]{1,0:T(8,128)(2,1)S(1)}, u32[]{:S(2)}, u32[]{:S(2)}) collective-permute-start(bf16[512,512]{1,0:T(8,128)(2,1)S(1)} %get-tuple-element.18.refs_0_), channel_id=1, source_target_pairs={{0,2},{2,0},{4,6},{6,4},{8,10},{10,8},{12,14},{14,12},{1,3},{3,1},... | collective-permute-start | bytes 1572872 | tf_op jit(solution)/shard_map/ppermute | solution.py:106
  209.7 32.2 %collective-permute-start.33 = (bf16[512,512]{1,0:T(8,128)(2,1)S(1)}, bf16[512,512]{1,0:T(8,128)(2,1)S(1)}, u32[]{:S(2)}, u32[]{:S(2)}) collective-permute-start(bf16[512,512]{1,0:T(8,128)(2,1)S(1)} %get-tuple-element.18.refs_0_), channel_id=1, source_target_pairs={{0,8},{2,10},{4,12},{6,14},{8,0},{10,2},{12,4},{14,6},{1,9},{3,11}... | collective-permute-start | bytes 1572872 | tf_op jit(solution)/shard_map/ppermute | solution.py:106
  213.9 42.8 %collective-permute-start.39 = (bf16[2,512,512]{2,1,0:T(8,128)(2,1)}, bf16[2,512,512]{2,1,0:T(8,128)(2,1)}, u32[]{:S(2)}, u32[]{:S(2)}) collective-permute-start(bf16[2,512,512]{2,1,0:T(8,128)(2,1)} %shard_map.18.refs_8_), channel_id=1, source_target_pairs={{0,16},{16,0},{1,17},{17,1},{2,18},{18,2},{3,19},{19,3},{4,20},{20... | collective-permute-start | bytes 3145736 | tf_op jit(solution)/shard_map/ppermute | solution.py:106
  241.3 22.1 %collective-permute-start.40 = (bf16[2,512,512]{2,1,0:T(8,128)(2,1)}, bf16[2,512,512]{2,1,0:T(8,128)(2,1)}, u32[]{:S(2)}, u32[]{:S(2)}) collective-permute-start(bf16[2,512,512]{2,1,0:T(8,128)(2,1)} %collective-permute-done.30.refs_9_), channel_id=1, source_target_pairs={{0,16},{16,0},{1,17},{17,1},{2,18},{18,2},{3,19},{19,3},{4,20},{20... | collective-permute-start | bytes 3145736 | tf_op jit(solution)/shard_map/ppermute | solution.py:106
  241.9 23.0 %collective-permute-start.29 = (bf16[2,512,512]{2,1,0:T(8,128)(2,1)}, bf16[2,512,512]{2,1,0:T(8,128)(2,1)}, u32[]{:S(2)}, u32[]{:S(2)}) collective-permute-start(bf16[2,512,512]{2,1,0:T(8,128)(2,1)} %shard_map.18.refs_8_), channel_id=1, source_target_pairs={{0,1},{1,0},{2,3},{3,2},{4,5},{5,4},{6,7},{7,6},{8,9},{9,8},{10,11... | collective-permute-start | bytes 3145736 | tf_op jit(solution)/shard_map/ppermute | solution.py:106
  242.7 26.2 %collective-permute-start.31 = (bf16[2,512,512]{2,1,0:T(8,128)(2,1)}, bf16[2,512,512]{2,1,0:T(8,128)(2,1)}, u32[]{:S(2)}, u32[]{:S(2)}) collective-permute-start(bf16[2,512,512]{2,1,0:T(8,128)(2,1)} %collective-permute-done.30.refs_9_), channel_id=1, source_target_pairs={{0,1},{1,0},{2,3},{3,2},{4,5},{5,4},{6,7},{7,6},{8,9},{9,8},{10,11... | collective-permute-start | bytes 3145736 | tf_op jit(solution)/shard_map/ppermute | solution.py:106
  256.6 35.5 %collective-permute-start.41 = (bf16[2,512,512]{2,1,0:T(8,128)(2,1)}, bf16[2,512,512]{2,1,0:T(8,128)(2,1)}, u32[]{:S(2)}, u32[]{:S(2)}) collective-permute-start(bf16[2,512,512]{2,1,0:T(8,128)(2,1)} %collective-permute-done.39.refs_10_), channel_id=1, source_target_pairs={{0,1},{1,0},{2,3},{3,2},{4,5},{5,4},{6,7},{7,6},{8,9},{9,8},{10,11... | collective-permute-start | bytes 3145736 | tf_op jit(solution)/shard_map/ppermute | solution.py:106
  263.5 39.7 %collective-permute-start.42 = (bf16[2,512,512]{2,1,0:T(8,128)(2,1)}, bf16[2,512,512]{2,1,0:T(8,128)(2,1)}, u32[]{:S(2)}, u32[]{:S(2)}) collective-permute-start(bf16[2,512,512]{2,1,0:T(8,128)(2,1)} %collective-permute-done.40.refs_12_), channel_id=1, source_target_pairs={{0,1},{1,0},{2,3},{3,2},{4,5},{5,4},{6,7},{7,6},{8,9},{9,8},{10,11... | collective-permute-start | bytes 3145736 | tf_op jit(solution)/shard_map/ppermute | solution.py:106
  264.9 15.9 %collective-permute-start.34 = (bf16[512,512]{1,0:T(8,128)(2,1)S(1)}, bf16[512,512]{1,0:T(8,128)(2,1)S(1)}, u32[]{:S(2)}, u32[]{:S(2)}) collective-permute-start(bf16[512,512]{1,0:T(8,128)(2,1)S(1)} %copy-done.11), channel_id=1, source_target_pairs={{0,2},{2,0},{4,6},{6,4},{8,10},{10,8},{12,14},{14,12},{1,3},{3,1},... | collective-permute-start | bytes 1572872 | tf_op jit(solution)/shard_map/ppermute | solution.py:106
  268.1 24.0 %collective-permute-start.36 = (bf16[512,512]{1,0:T(8,128)(2,1)}, bf16[512,512]{1,0:T(8,128)(2,1)S(1)}, u32[]{:S(2)}, u32[]{:S(2)}) collective-permute-start(bf16[512,512]{1,0:T(8,128)(2,1)} %collective-permute-done.35.refs_4_), channel_id=1, source_target_pairs={{0,2},{2,0},{4,6},{6,4},{8,10},{10,8},{12,14},{14,12},{1,3},{3,1},... | collective-permute-start | bytes 1572872 | tf_op jit(solution)/shard_map/ppermute | solution.py:106
  269.0 34.2 %collective-permute-start.38 = (bf16[512,512]{1,0:T(8,128)(2,1)}, bf16[512,512]{1,0:T(8,128)(2,1)S(1)}, u32[]{:S(2)}, u32[]{:S(2)}) collective-permute-start(bf16[512,512]{1,0:T(8,128)(2,1)} %collective-permute-done.37.refs_6_), channel_id=1, source_target_pairs={{0,2},{2,0},{4,6},{6,4},{8,10},{10,8},{12,14},{14,12},{1,3},{3,1},... | collective-permute-start | bytes 1572872 | tf_op jit(solution)/shard_map/ppermute | solution.py:106
  (29 other events, 311.2 us)

commit v2 on v1

v2 whole, which is shorter than its diff:
```python
import functools
import math

import jax
import jax.numpy as jnp
from jax import lax
from jax.experimental import pallas as pl
from jax.experimental.pallas import tpu as pltpu
from jax.sharding import PartitionSpec as P


def fast_length(mesh):
    count = mesh.shape["row"]
    line = mesh.devices.reshape(mesh.shape["seg"], count, mesh.shape["col"])[0, :, 0]
    coords = [getattr(d, "coords", None) for d in line]
    if count < 2 or any(c is None for c in coords):
        return 1
    moving = [a for a in range(len(coords[0])) if coords[0][a] != coords[1][a]]
    if len(moving) != 1:
        return 1
    length = 1
    while length < count and all(
        coords[length][a] == coords[0][a] for a in range(len(coords[0])) if a != moving[0]
    ):
        length += 1
    return length if count % length == 0 else 1


def after(value, *others):
    return lax.optimization_barrier((value, *others))[0]


def product_kernel(n_left, n_right, by_half, earlier, scale, place, *refs):
    left, refs = refs[:n_left], refs[n_left:]
    right, refs = refs[:n_right], refs[n_right:]
    before, refs = refs[:earlier], refs[earlier:]
    *outs, lscr, rscr, acc, lsem, rsem, asem = refs
    halves, _, subs, cores, _, _ = rscr.shape

    def right_copy(i):
        y, s, c = place[1, i], place[2, i], place[3, i]
        target = rscr.at[s, y, :, c] if by_half else rscr.at[0, y, s, c]
        return pltpu.make_async_copy(right[i], target, rsem.at[y, s, c])

    for i in range(n_right):
        pl.when(place[4, i] == 1)(right_copy(i).start)
    for i in range(n_left):
        pltpu.make_async_copy(left[i], lscr.at[i], lsem.at[i]).start()
    copies = [pltpu.make_async_copy(b, acc.at[h], asem.at[h]) for h, b in enumerate(before)]
    for copy in copies:
        copy.start()
    for copy in copies:
        copy.wait()
    if by_half:
        for i in range(n_right):
            pl.when(place[4, i] == 1)(right_copy(i).wait)
    for i in range(n_left):
        k = place[0, i]
        y, s, c = k // (subs * cores), (k // cores) % subs, k % cores
        pltpu.make_async_copy(left[i], lscr.at[i], lsem.at[i]).wait()
        if not by_half:
            pltpu.make_async_copy(right[0], rscr.at[0, y, s, c], rsem.at[y, s, c]).wait()
        for h in range(halves):
            term = jnp.dot(lscr[i], rscr[h, y, s, c], preferred_element_type=jnp.float32)
            if i or earlier:
                term += acc[h]
            if i < n_left - 1:
                acc[h] = term
            else:
                outs[h][...] = (term * scale).astype(outs[h].dtype)


def product(left, right, before, by_half, scale, segs, place, final):
    q, w = left[0].shape
    n_left, n_right = len(left), len(right)
    halves = 2 if by_half else 1

    def body(place_ref, *refs):
        product_kernel(n_left, n_right, by_half, len(before), scale, place_ref, *refs)

    return pl.pallas_call(
        body,
        out_shape=[jax.ShapeDtypeStruct((q, w), jnp.bfloat16 if final else jnp.float32)] * halves,
        in_specs=[pl.BlockSpec(memory_space=pltpu.SMEM)]
        + [pl.BlockSpec(memory_space=pl.ANY)] * (n_left + n_right + len(before)),
        out_specs=[pl.BlockSpec(memory_space=pltpu.VMEM)] * halves,
        scratch_shapes=[
            pltpu.VMEM((n_left, q, w), jnp.bfloat16),
            pltpu.VMEM((halves, segs, 2, 2, q, w), jnp.bfloat16),
            pltpu.VMEM((halves, q, w), jnp.float32),
            pltpu.SemaphoreType.DMA((n_left,)),
            pltpu.SemaphoreType.DMA((segs, 2, 2)),
            pltpu.SemaphoreType.DMA((halves,)),
        ],
        cost_estimate=pl.CostEstimate(
            flops=2 * halves * q * n_left * w * w, bytes_accessed=2 * n_left * w * (q + halves * w), transcendentals=0
        ),
        compiler_params=pltpu.CompilerParams(vmem_limit_bytes=40 << 20),
    )(place, *left, *right, *before)


def local(fast, slices):
    segs, rows, _ = (lax.axis_size(a) for a in ("seg", "row", "col"))
    slow = rows // fast
    height, w = slices.shape[1:]
    q = height // 4
    y, r, c = (lax.axis_index(a) for a in ("seg", "row", "col"))
    z, x = r // fast, r % fast
    zl = z % 2
    factor = math.sqrt(segs * height)

    def send(value, axes, pairs, gate=None):
        if gate is not None:
            value = after(value, gate)
        return lax.ppermute(value, axes, pairs)

    def along(value, dz, dx, gate=None):
        pairs = [
            (i, ((i // fast + dz) % slow) * fast + (i % fast + dx) % fast) for i in range(rows)
        ]
        return send(value, "row", pairs, gate)

    def seg_shift(value, dy, gate=None):
        return send(value, "seg", [(i, (i + dy) % segs) for i in range(segs)], gate)

    def partner(i):
        return ((i // fast) ^ 1) * fast + i % fast

    def plane_swap(value, gate=None):
        return send(value, "row", [(i, partner(i)) for i in range(rows)], gate)

    def core_swap(value):
        return send(value, "col", [(0, 1), (1, 0)])

    def row_half(block, i):
        return lax.dynamic_index_in_dim(block, i, 0, keepdims=False)

    class Left:
        def __init__(self, block):
            self.same, self.other = row_half(block, zl), row_half(block, 1 - zl)
            self.pieces = []

        def over_slow(self, j, gate=None):
            piece = along(self.same if j % 2 == 0 else self.other, j, 0, gate)
            return j, piece

        def over_fast(self, j_piece):
            j, piece = j_piece
            self.pieces.append((j, 0, piece))
            for i in range(1, fast):
                self.pieces.append((j, i, along(piece, 0, i)))

        def places(self):
            return [((z - j) % slow) * fast + (x - i) % fast for j, i, _ in self.pieces]

    class Right:
        def __init__(self, block):
            self.pieces = [(0, 0, 0, block)]

        def places(self):
            return [
                [(y - dy) % segs for dy, _, _, _ in self.pieces],
                [zl ^ s for _, s, _, _ in self.pieces],
                [c ^ k for _, _, k, _ in self.pieces],
            ]

        def add(self, key, block):
            self.pieces.append((*key, block))
            return block

        def block(self, *key):
            return [p[-1] for p in self.pieces if p[:3] == key][0]

        def plane(self, gate=None):
            return self.add((0, 1, 0), plane_swap(self.block(0, 0, 0), gate))

        def segs(self, s, gate=None):
            block = self.block(0, s, 0)
            return [self.add((dy, s, 0), seg_shift(block, dy, gate)) for dy in range(1, segs)]

        def cross(self, s, others=False):
            for dy in range(1, segs) if others else [0]:
                self.add((dy, s, 1), core_swap(self.block(dy, s, 0)))

    def part(left, chosen, right, before, by_half, scale, final):
        places = [left.places()[i] for i in chosen]
        table = [places] + right.places()
        flags = []
        for ry, rs, rc in zip(*table[1:]):
            match = lambda k: (k // 4 == ry) & (k % 2 == rc) & (by_half | (k // 2 % 2 == rs))
            flags.append(functools.reduce(jnp.logical_or, [match(k) for k in places]))
        table.append(flags)
        width = max(len(t) for t in table)
        zero = jnp.int32(0)
        place = jnp.stack(
            [jnp.stack([jnp.asarray(v, jnp.int32) for v in t] + [zero] * (width - len(t))) for t in table]
        )
        return product(
            [left.pieces[i][-1] for i in chosen],
            [p[-1] for p in right.pieces],
            before,
            by_half,
            scale,
            segs,
            place,
            final,
        )

    def own_block(halves):
        found = {
            (t, k): jnp.where(zl == 0, *(right.block(0, t, k) for right in halves))
            for t in range(2)
            for k in range(2)
        }

        def pick(s, k):
            by_core = [jnp.where(c == k, found[(t, 0)], found[(t, 1)]) for t in range(2)]
            return jnp.where(zl == s, by_core[0], by_core[1])

        return jnp.stack([jnp.stack([pick(s, k) for k in range(2)]) for s in range(2)])

    evens, odds = range(2, slow, 2), range(1, slow, 2)

    parts = slices.reshape(2, 2, 2, q, w)
    theirs = [core_swap(jnp.where(c == 0, parts[0, :, 1], parts[0, :, 0]))]
    right = Right(jnp.where(c == 0, parts[0, :, 0], theirs[0]))
    plane = right.plane()
    given = after(parts[1], right.block(0, 0, 0))
    theirs.append(core_swap(jnp.where(c == 0, given[:, 1], given[:, 0])))
    right.segs(0)
    left = Left(jnp.where(c == 0, parts[1, :, 0], theirs[1]))
    coming = [left.over_slow(j) for j in evens]
    left.over_fast((0, left.same))
    theirs = after(theirs, left.same)
    left2 = Left(jnp.where(c == 0, theirs[0], parts[0, :, 1]))
    left3 = Left(jnp.where(c == 0, theirs[1], parts[1, :, 1]))
    right.cross(0)
    coming.append(left.over_slow(odds[0]))
    left2.over_fast((0, left2.same))
    left3.over_fast((0, left3.same))
    coming += [left.over_slow(j) for j in odds[1:]]
    for earlier in coming[: len(evens)]:
        left.over_fast(earlier)
    right.segs(1)
    early = [left2.over_slow(j) for j in (*evens, *odds)]
    right.cross(1)
    right.cross(0, others=True)
    for earlier in coming[len(evens) : -1]:
        left.over_fast(earlier)
    rest = len(left.pieces)
    left.over_fast(coming[-1])
    rest += 1
    right.cross(1, others=True)
    ready = part(left, range(rest), right, [], True, 1.0, fast == 1)
    if fast > 1:
        ready = part(left, range(rest, len(left.pieces)), right, ready, True, 1.0, True)

    a, b = Right(ready[0]), Right(ready[1])
    plane = a.plane()
    a.segs(0)
    a.cross(0)
    b.plane()
    for item in early[:-1]:
        left2.over_fast(item)
    a.segs(1)
    b.segs(0)
    b.cross(0)
    a.cross(1)
    a.cross(0, others=True)
    left2.over_fast(early[-1])
    early3 = [left3.over_slow(j) for j in (*evens, *odds)]
    b.segs(1)
    a.cross(1, others=True)
    (ready_a,) = part(left2, range(len(left2.pieces)), a, [], False, 1.0, True)
    a3 = Right(ready_a)
    a3.plane()
    a3.segs(0)
    a3.cross(0)
    b.cross(0, others=True)
    b.cross(1)
    left3.over_fast(early3[0])
    b.cross(1, others=True)
    (ready_b,) = part(left2, range(len(left2.pieces)), b, [], False, 1.0, True)
    b3 = Right(ready_b)

    b3.plane()
    b3.segs(0)
    b3.cross(0)
    for item in early3[1:]:
        left3.over_fast(item)
    a3.segs(1)
    a3.cross(1)
    a3.cross(0, others=True)
    b3.segs(1)
    a3.cross(1, others=True)
    (last_a,) = part(left3, range(len(left3.pieces)), a3, [], False, factor, True)

    def home(h, value):
        slots = [i * 2 + k for i in range(rows) for k in range(2) if (i // fast) % 2 != h]
        moved = [
            send(value, ("row", "col"), [(i, partner(i // 2) * 2 + 1) for i in slots if i % 2 == k])
            for k in range(2)
        ]
        slots = [i for i in range(rows) if (i // fast) % 2 == h]
        kept = send(value, ("row", "col"), [(i * 2, i * 2 + 1) for i in slots])
        return kept, moved

    kept_a, moved_a = home(0, last_a)
    b3.cross(1)
    b3.cross(0, others=True)
    b3.cross(1, others=True)
    (last_b,) = part(left3, range(len(left3.pieces)), b3, [], False, factor, True)
    kept_b, moved_b = home(1, last_b)
    here = jnp.where(zl == 0, jnp.stack([kept_a, last_a]), jnp.stack([kept_b, last_b]))
    there = jnp.where(zl == 0, jnp.stack(moved_a), jnp.stack(moved_b))
    final = jnp.stack([jnp.where(zl == s, here, there) for s in range(2)])

    def scaled(value):
        return (value.astype(jnp.float32) * factor).astype(jnp.bfloat16)

    for item in (a, b, a3, b3):
        item.pieces = [(*p[:3], after(p[3], last_b)) for p in item.pieces]
    head = jnp.where(c == 0, slices[0].reshape(2, 2, q, w), own_block((a3, b3)))
    tail = jnp.where(c == 0, scaled(own_block((a, b))), final)
    return jnp.stack([scaled(head).reshape(height, w), tail.reshape(height, w)], axis=0)


def solution(mesh):
    spec = P("col", "seg", "row")
    fast = fast_length(mesh)

    def body(slices):
        return local(fast, slices)

    return jax.shard_map(body, mesh=mesh, in_specs=(spec,), out_specs=spec, check_vma=False)
```

time: 330 us -> 384 us (1.16); the launches traced: 328 us -> 377 us
  local copies, waits for them, and re-layouts: 13.4 us -> 51.2 us
  waiting for transfers between devices: 223 us -> 196 us
  starting transfers between devices: 56.7 us -> 82.9 us
  Pallas kernels: 23.2 us -> 30.5 us
    unnamed x30 -> x134, local copies, waits for them, and re-layouts: 9.01 us -> 47.3 us
    ppermute x46 -> x64, waiting for transfers between devices: 223 us -> 196 us  [send(): return lax.ppermute(value, axes, pairs)]
    ppermute x46 -> x64, starting transfers between devices: 56.7 us -> 82.9 us  [send(): return lax.ppermute(value, axes, pairs)]
    pallas_call x3 -> x6, Pallas kernels: 23.2 us -> 30.5 us  [product(): pl.pallas_call(body, out_shape=[jax.ShapeDtypeStruct((q, w), jnp.bfloat16...]
    select_n x5 -> x7, other arithmetic: 7.84 us -> 8.58 us  [the longest x1 1.74 us: local(): right = Right(jnp.where(c == 0, parts[0, :, 0], theirs[0]))]
  transfers between devices with their start and end apart: 46 -> 64, of which waited for: 23 -> 21; matrix products, arithmetic and copies ran while one was open for 2% -> 3% of each run, Pallas kernels for 0% -> 8%
where the time goes in v2:
time: 384 us; the launch traced here: 377 us
  waiting for transfers between devices  196 us (51%)
  starting transfers between devices  82.9 us (22%)
  local copies, waits for them, and re-layouts  51.2 us (13%)
  Pallas kernels  30.5 us (8%)
  other arithmetic  14.5 us (4%)
    ppermute x64, waiting for transfers between devices, send(): return lax.ppermute(value, axes, pairs)  196 us
    ppermute x64, starting transfers between devices, send(): return lax.ppermute(value, axes, pairs)  82.9 us
    unnamed x134, local copies, waits for them, and re-layouts  47.3 us
    pallas_call x6, Pallas kernels, product(): pl.pallas_call(body, out_shape=[jax.ShapeDtypeStruct((q, w), jnp.bfloat16...  30.5 us
  transfers between devices with their start and end apart: 64, of which 21 were waited for; matrix products, arithmetic and copies ran while one was open for 3% of the time, Pallas kernels for 8%

profile of v2, /device:TPU:0, one launch (start us, length us, event | category | flops | bytes accessed | tf_op | source)
XLA Modules:
  0.0 376.8 jit_solution(10048164138507523456)
XLA Ops:
  7.9 2.7 collective-permute-start.11
  13.7 3.7 collective-permute-start.9
  18.9 15.8 %collective-permute-done.11.refs_8_.refs_2_ = bf16[2,512,512]{2,1,0:T(8,128)(2,1)} collective-permute-done((bf16[2,512,512]{2,1,0:T(8,128)(2,1)S(1)}, bf16[2,512,512]{2,1,0:T(8,128)(2,1)}, u32[]{:S(2)}, u32[]{:S(2)}) %collective-permute-start.11) | collective-permute-done | bytes 1048608 | tf_op jit(solution)/shard_map/ppermute | solution.py:115
  34.7 3.0 collective-permute-start.19
  42.5 12.2 %collective-permute-start.21 = (bf16[512,512]{1,0:T(8,128)(2,1)S(1)}, bf16[512,512]{1,0:T(8,128)(2,1)}, u32[]{:S(2)}, u32[]{:S(2)}) collective-permute-start(bf16[512,512]{1,0:T(8,128)(2,1)S(1)} %get-tuple-element.78), channel_id=1, source_target_pairs={{0,4},{2,6},{4,8},{6,10},{8,12},{10,14},{12,0},{14,2},{1,5},{3,7},... | collective-permute-start | bytes 1572872 | tf_op jit(solution)/shard_map/ppermute | solution.py:115
  55.8 50.6 %collective-permute-done.19.refs_2_ = bf16[512,512]{1,0:T(8,128)(2,1)} collective-permute-done((bf16[512,512]{1,0:T(8,128)(2,1)S(1)}, bf16[512,512]{1,0:T(8,128)(2,1)}, u32[]{:S(2)}, u32[]{:S(2)}) %collective-permute-start.19) | collective-permute-done | bytes 524320 | tf_op jit(solution)/shard_map/ppermute | solution.py:115
  106.6 11.0 %collective-permute-done.31.refs_2_ = bf16[512,512]{1,0:T(8,128)(2,1)S(1)} collective-permute-done((bf16[512,512]{1,0:T(8,128)(2,1)S(1)}, bf16[512,512]{1,0:T(8,128)(2,1)S(1)}, u32[]{:S(2)}, u32[]{:S(2)}) %collective-permute-start.31) | collective-permute-done | bytes 524320 | tf_op jit(solution)/shard_map/ppermute | solution.py:115
  117.5 7.7 %collective-permute-start.5 = (bf16[512,512]{1,0:T(8,128)(2,1)S(1)}, bf16[512,512]{1,0:T(8,128)(2,1)}, u32[]{:S(2)}, u32[]{:S(2)}) collective-permute-start(bf16[512,512]{1,0:T(8,128)(2,1)S(1)} %get-tuple-element.73), channel_id=1, source_target_pairs={{0,4},{2,6},{4,8},{6,10},{8,12},{10,14},{12,0},{14,2},{1,5},{3,7},... | collective-permute-start | bytes 1572872 | tf_op jit(solution)/shard_map/ppermute | solution.py:115
  125.2 13.6 %collective-permute-done.3.refs_2_ = bf16[512,512]{1,0:T(8,128)(2,1)S(1)} collective-permute-done((bf16[512,512]{1,0:T(8,128)(2,1)S(1)}, bf16[512,512]{1,0:T(8,128)(2,1)S(1)}, u32[]{:S(2)}, u32[]{:S(2)}) %collective-permute-start.3) | collective-permute-done | bytes 524320 | tf_op jit(solution)/shard_map/ppermute | solution.py:115
  143.9 9.3 %collective-permute-start.35 = (bf16[512,512]{1,0:T(8,128)(2,1)}, bf16[512,512]{1,0:T(8,128)(2,1)}, u32[]{:S(2)}, u32[]{:S(2)}) collective-permute-start(bf16[512,512]{1,0:T(8,128)(2,1)} %get-tuple-element.75), channel_id=1, source_target_pairs={{0,12},{2,14},{4,0},{6,2},{8,4},{10,6},{12,8},{14,10},{1,13},{3,15... | collective-permute-start | bytes 1572872 | tf_op jit(solution)/shard_map/ppermute | solution.py:115
  156.1 9.9 %collective-permute-done.20.refs_3_ = bf16[512,512]{1,0:T(8,128)(2,1)} collective-permute-done((bf16[512,512]{1,0:T(8,128)(2,1)}, bf16[512,512]{1,0:T(8,128)(2,1)}, u32[]{:S(2)}, u32[]{:S(2)}) %collective-permute-start.20) | collective-permute-done | bytes 524320 | tf_op jit(solution)/shard_map/ppermute | solution.py:115
  166.0 11.2 %collective-permute-done.22.refs_5_ = bf16[512,512]{1,0:T(8,128)(2,1)} collective-permute-done((bf16[512,512]{1,0:T(8,128)(2,1)}, bf16[512,512]{1,0:T(8,128)(2,1)}, u32[]{:S(2)}, u32[]{:S(2)}) %collective-permute-start.22) | collective-permute-done | bytes 524320 | tf_op jit(solution)/shard_map/ppermute | solution.py:115
  182.6 7.9 %shard_map.17 = (f32[512,512]{1,0:T(8,128)S(1)}, f32[512,512]{1,0:T(8,128)S(1)}) custom-call(s32[5,8]{1,0:T(8,128)S(1)} %stack.282.place_ref, bf16[512,512]{1,0:T(8,128)(2,1)S(1)} %copy-done.59, bf16[512,512]{1,0:T(8,128)(2,1)S(1)} %copy-done.61, bf16[512,512]{1,0:T(8,128)(2,1)} %collective-permute-done.19.refs_2_, ...), custom_call_target="tpu_custom_call" | custom-call | flops 3758096384 | bytes 11010048 | tf_op jit(solution)/shard_map/pallas_call | solution.py:81
  190.5 2.9 shard_map.18
  196.8 2.7 collective-permute-done.4.refs_3_
  201.8 9.0 %collective-permute-done.6.refs_5_ = bf16[512,512]{1,0:T(8,128)(2,1)S(1)} collective-permute-done((bf16[512,512]{1,0:T(8,128)(2,1)}, bf16[512,512]{1,0:T(8,128)(2,1)S(1)}, u32[]{:S(2)}, u32[]{:S(2)}) %collective-permute-start.6) | collective-permute-done | bytes 524320 | tf_op jit(solution)/shard_map/ppermute | solution.py:115
  212.4 7.6 %collective-permute-done.8.refs_7_ = bf16[512,512]{1,0:T(8,128)(2,1)S(1)} collective-permute-done((bf16[512,512]{1,0:T(8,128)(2,1)}, bf16[512,512]{1,0:T(8,128)(2,1)S(1)}, u32[]{:S(2)}, u32[]{:S(2)}) %collective-permute-start.8) | collective-permute-done | bytes 524320 | tf_op jit(solution)/shard_map/ppermute | solution.py:115
  228.7 7.1 %collective-permute-done.24.refs_10_ = bf16[512,512]{1,0:T(8,128)(2,1)} collective-permute-done((bf16[512,512]{1,0:T(8,128)(2,1)S(1)}, bf16[512,512]{1,0:T(8,128)(2,1)}, u32[]{:S(2)}, u32[]{:S(2)}) %collective-permute-start.24) | collective-permute-done | bytes 524320 | tf_op jit(solution)/shard_map/ppermute | solution.py:115
  236.6 10.3 %collective-permute-done.40.refs_12_ = bf16[512,512]{1,0:T(8,128)(2,1)S(1)} collective-permute-done((bf16[512,512]{1,0:T(8,128)(2,1)S(1)}, bf16[512,512]{1,0:T(8,128)(2,1)S(1)}, u32[]{:S(2)}, u32[]{:S(2)}) %collective-permute-start.40) | collective-permute-done | bytes 524320 | tf_op jit(solution)/shard_map/ppermute | solution.py:115
  249.0 8.8 %collective-permute-done.26.refs_12_ = bf16[512,512]{1,0:T(8,128)(2,1)} collective-permute-done((bf16[512,512]{1,0:T(8,128)(2,1)S(1)}, bf16[512,512]{1,0:T(8,128)(2,1)}, u32[]{:S(2)}, u32[]{:S(2)}) %collective-permute-start.26) | collective-permute-done | bytes 524320 | tf_op jit(solution)/shard_map/ppermute | solution.py:115
  277.4 4.6 %shard_map.20.refs_8_ = bf16[512,512]{1,0:T(8,128)(2,1)S(1)} custom-call(s32[5,8]{1,0:T(8,128)S(1)} %stack.289.place_ref, bf16[512,512]{1,0:T(8,128)(2,1)S(1)} %get-tuple-element.74.refs_0_, bf16[512,512]{1,0:T(8,128)(2,1)} %collective-permute-done.2.refs_1_, bf16[512,512]{1,0:T(8,128)(2,1)S(1)} %copy-done.1, bf16[512,512]{1,0:T(8,128)(2,1)S(1)} %copy-done.28, ...), custom_call_target="tpu_custom_call" | custom-call | flops 2147483648 | bytes 8388608 | tf_op jit(solution)/shard_map/pallas_call | solution.py:81
  291.1 5.0 %shard_map.19.refs_8_ = bf16[512,512]{1,0:T(8,128)(2,1)S(1)} custom-call(s32[5,8]{1,0:T(8,128)S(1)} %stack.262.place_ref, bf16[512,512]{1,0:T(8,128)(2,1)S(1)} %get-tuple-element.74.refs_0_, bf16[512,512]{1,0:T(8,128)(2,1)} %collective-permute-done.2.refs_1_, bf16[512,512]{1,0:T(8,128)(2,1)S(1)} %copy-done.2, bf16[512,512]{1,0:T(8,128)(2,1)S(1)} %copy-done.29, ...), custom_call_target="tpu_custom_call" | custom-call | flops 2147483648 | bytes 8388608 | tf_op jit(solution)/shard_map/pallas_call | solution.py:81
  297.7 2.1 collective-permute-start.52
  300.2 6.4 %collective-permute-done.36.refs_7_ = bf16[512,512]{1,0:T(8,128)(2,1)S(1)} collective-permute-done((bf16[512,512]{1,0:T(8,128)(2,1)}, bf16[512,512]{1,0:T(8,128)(2,1)S(1)}, u32[]{:S(2)}, u32[]{:S(2)}) %collective-permute-start.36) | collective-permute-done | bytes 524320 | tf_op jit(solution)/shard_map/ppermute | solution.py:115
  314.6 7.7 %collective-permute-done.47.refs_12_ = bf16[512,512]{1,0:T(8,128)(2,1)} collective-permute-done((bf16[512,512]{1,0:T(8,128)(2,1)}, bf16[512,512]{1,0:T(8,128)(2,1)}, u32[]{:S(2)}, u32[]{:S(2)}) %collective-permute-start.47) | collective-permute-done | bytes 524320 | tf_op jit(solution)/shard_map/ppermute | solution.py:115
  322.3 11.2 %collective-permute-done.54.refs_10_ = bf16[512,512]{1,0:T(8,128)(2,1)} collective-permute-done((bf16[512,512]{1,0:T(8,128)(2,1)S(1)}, bf16[512,512]{1,0:T(8,128)(2,1)}, u32[]{:S(2)}, u32[]{:S(2)}) %collective-permute-start.54) | collective-permute-done | bytes 524320 | tf_op jit(solution)/shard_map/ppermute | solution.py:115
  335.6 7.5 %collective-permute-done.55.refs_12_ = bf16[512,512]{1,0:T(8,128)(2,1)} collective-permute-done((bf16[512,512]{1,0:T(8,128)(2,1)}, bf16[512,512]{1,0:T(8,128)(2,1)}, u32[]{:S(2)}, u32[]{:S(2)}) %collective-permute-start.55) | collective-permute-done | bytes 524320 | tf_op jit(solution)/shard_map/ppermute | solution.py:115
  348.4 4.7 %shard_map.21 = bf16[512,512]{1,0:T(8,128)(2,1)S(1)} custom-call(s32[5,8]{1,0:T(8,128)S(1)} %stack.262.place_ref, bf16[512,512]{1,0:T(8,128)(2,1)S(1)} %get-tuple-element.76.refs_0_, bf16[512,512]{1,0:T(8,128)(2,1)} %collective-permute-done.30.refs_1_, bf16[512,512]{1,0:T(8,128)(2,1)S(1)} %collective-permute-done.31.refs_2_, ...), custom_call_target="tpu_custom_call" | custom-call | flops 2147483648 | bytes 8388608 | tf_op jit(solution)/shard_map/pallas_call | solution.py:81
  354.1 4.5 %collective-permute-start.62 = (bf16[512,512]{1,0:T(8,128)(2,1)S(1)}, bf16[512,512]{1,0:T(8,128)(2,1)S(1)}, u32[]{:S(2)}, u32[]{:S(2)}) collective-permute-start(bf16[512,512]{1,0:T(8,128)(2,1)S(1)} %shard_map.21), channel_id=1, source_target_pairs={{0,5},{2,7},{8,13},{10,15},{16,21},{18,23},{24,29},{26,31}} | collective-permute-start | bytes 1572872 | tf_op jit(solution)/shard_map/ppermute | solution.py:115
  358.6 5.4 %shard_map.22 = bf16[512,512]{1,0:T(8,128)(2,1)S(1)} custom-call(s32[5,8]{1,0:T(8,128)S(1)} %stack.262.place_ref, bf16[512,512]{1,0:T(8,128)(2,1)S(1)} %get-tuple-element.76.refs_0_, bf16[512,512]{1,0:T(8,128)(2,1)} %collective-permute-done.30.refs_1_, bf16[512,512]{1,0:T(8,128)(2,1)S(1)} %collective-permute-done.31.refs_2_, ...), custom_call_target="tpu_custom_call" | custom-call | flops 2147483648 | bytes 8388608 | tf_op jit(solution)/shard_map/pallas_call | solution.py:81
  369.0 2.9 collective-permute-start.58
  374.5 2.4 pad_maximum_fusion
  (279 shorter events, 104.0 us)
Async XLA Ops:
  7.9 26.8 %collective-permute-start.11 = (bf16[2,512,512]{2,1,0:T(8,128)(2,1)S(1)}, bf16[2,512,512]{2,1,0:T(8,128)(2,1)}, u32[]{:S(2)}, u32[]{:S(2)}) collective-permute-start(bf16[2,512,512]{2,1,0:T(8,128)(2,1)S(1)} %broadcast_select_fusion.3.refs_7_.refs_1_), channel_id=1, source_target_pairs={{0,4},{2,6},{4,0},{6,2},{8,12},{10,14},{12,8},{14,10},{1,5},{3,7},... | collective-permute-start | bytes 3145736 | tf_op jit(solution)/shard_map/ppermute | solution.py:115
  10.6 27.2 %collective-permute-start.12 = (bf16[2,512,512]{2,1,0:T(8,128)(2,1)S(1)}, bf16[2,512,512]{2,1,0:T(8,128)(2,1)}, u32[]{:S(2)}, u32[]{:S(2)}) collective-permute-start(bf16[2,512,512]{2,1,0:T(8,128)(2,1)S(1)} %broadcast_select_fusion.3.refs_7_.refs_1_), channel_id=1, source_target_pairs={{0,16},{16,0},{1,17},{17,1},{2,18},{18,2},{3,19},{19,3},{4,20},{20... | collective-permute-start | bytes 3145736 | tf_op jit(solution)/shard_map/ppermute | solution.py:115
  12.1 29.5 %collective-permute-start.13 = (bf16[2,512,512]{2,1,0:T(8,128)(2,1)S(1)}, bf16[2,512,512]{2,1,0:T(8,128)(2,1)S(1)}, u32[]{:S(2)}, u32[]{:S(2)}) collective-permute-start(bf16[2,512,512]{2,1,0:T(8,128)(2,1)S(1)} %broadcast_select_fusion.3.refs_7_.refs_1_), channel_id=1, source_target_pairs={{0,1},{1,0},{2,3},{3,2},{4,5},{5,4},{6,7},{7,6},{8,9},{9,8},{10,11... | collective-permute-start | bytes 3145736 | tf_op jit(solution)/shard_map/ppermute | solution.py:115
  13.7 42.0 %collective-permute-start.9 = (bf16[512,512]{1,0:T(8,128)(2,1)S(1)}, bf16[512,512]{1,0:T(8,128)(2,1)}, u32[]{:S(2)}, u32[]{:S(2)}) collective-permute-start(bf16[512,512]{1,0:T(8,128)(2,1)S(1)} %get-tuple-element.78), channel_id=1, source_target_pairs={{0,12},{2,14},{4,0},{6,2},{8,4},{10,6},{12,8},{14,10},{1,13},{3,15... | collective-permute-start | bytes 1572872 | tf_op jit(solution)/shard_map/ppermute | solution.py:115
  17.4 38.3 %collective-permute-start.18 = (bf16[512,512]{1,0:T(8,128)(2,1)S(1)}, bf16[512,512]{1,0:T(8,128)(2,1)S(1)}, u32[]{:S(2)}, u32[]{:S(2)}) collective-permute-start(bf16[512,512]{1,0:T(8,128)(2,1)S(1)} %get-tuple-element.77.refs_0_), channel_id=1, source_target_pairs={{0,2},{2,0},{4,6},{6,4},{8,10},{10,8},{12,14},{14,12},{1,3},{3,1},... | collective-permute-start | bytes 1572872 | tf_op jit(solution)/shard_map/ppermute | solution.py:115
  34.7 71.7 %collective-permute-start.19 = (bf16[512,512]{1,0:T(8,128)(2,1)S(1)}, bf16[512,512]{1,0:T(8,128)(2,1)}, u32[]{:S(2)}, u32[]{:S(2)}) collective-permute-start(bf16[512,512]{1,0:T(8,128)(2,1)S(1)} %get-tuple-element.77.refs_0_), channel_id=1, source_target_pairs={{0,8},{2,10},{4,12},{6,14},{8,0},{10,2},{12,4},{14,6},{1,9},{3,11}... | collective-permute-start | bytes 1572872 | tf_op jit(solution)/shard_map/ppermute | solution.py:115
  37.7 87.4 %collective-permute-start.14 = (bf16[2,512,512]{2,1,0:T(8,128)(2,1)}, bf16[2,512,512]{2,1,0:T(8,128)(2,1)}, u32[]{:S(2)}, u32[]{:S(2)}) collective-permute-start(bf16[2,512,512]{2,1,0:T(8,128)(2,1)} %collective-permute-done.11.refs_8_.refs_2_), channel_id=1, source_target_pairs={{0,16},{16,0},{1,17},{17,1},{2,18},{18,2},{3,19},{19,3},{4,20},{20... | collective-permute-start | bytes 3145736 | tf_op jit(solution)/shard_map/ppermute | solution.py:115
  42.5 63.9 %collective-permute-start.21 = (bf16[512,512]{1,0:T(8,128)(2,1)S(1)}, bf16[512,512]{1,0:T(8,128)(2,1)}, u32[]{:S(2)}, u32[]{:S(2)}) collective-permute-start(bf16[512,512]{1,0:T(8,128)(2,1)S(1)} %get-tuple-element.78), channel_id=1, source_target_pairs={{0,4},{2,6},{4,8},{6,10},{8,12},{10,14},{12,0},{14,2},{1,5},{3,7},... | collective-permute-start | bytes 1572872 | tf_op jit(solution)/shard_map/ppermute | solution.py:115
  55.7 61.8 %collective-permute-start.31 = (bf16[512,512]{1,0:T(8,128)(2,1)S(1)}, bf16[512,512]{1,0:T(8,128)(2,1)S(1)}, u32[]{:S(2)}, u32[]{:S(2)}) collective-permute-start(bf16[512,512]{1,0:T(8,128)(2,1)S(1)} %get-tuple-element.76.refs_0_), channel_id=1, source_target_pairs={{0,8},{2,10},{4,12},{6,14},{8,0},{10,2},{12,4},{14,6},{1,9},{3,11}... | collective-permute-start | bytes 1572872 | tf_op jit(solution)/shard_map/ppermute | solution.py:115
  55.7 61.8 %collective-permute-start.33 = (bf16[512,512]{1,0:T(8,128)(2,1)}, bf16[512,512]{1,0:T(8,128)(2,1)S(1)}, u32[]{:S(2)}, u32[]{:S(2)}) collective-permute-start(bf16[512,512]{1,0:T(8,128)(2,1)} %get-tuple-element.75), channel_id=1, source_target_pairs={{0,4},{2,6},{4,8},{6,10},{8,12},{10,14},{12,0},{14,2},{1,5},{3,7},... | collective-permute-start | bytes 1572872 | tf_op jit(solution)/shard_map/ppermute | solution.py:115
  106.4 36.0 %collective-permute-start.15 = (bf16[2,512,512]{2,1,0:T(8,128)(2,1)}, bf16[2,512,512]{2,1,0:T(8,128)(2,1)}, u32[]{:S(2)}, u32[]{:S(2)}) collective-permute-start(bf16[2,512,512]{2,1,0:T(8,128)(2,1)} %collective-permute-done.11.refs_8_.refs_2_), channel_id=1, source_target_pairs={{0,1},{1,0},{2,3},{3,2},{4,5},{5,4},{6,7},{7,6},{8,9},{9,8},{10,11... | collective-permute-start | bytes 3145736 | tf_op jit(solution)/shard_map/ppermute | solution.py:115
  106.5 32.4 %collective-permute-start.3 = (bf16[512,512]{1,0:T(8,128)(2,1)S(1)}, bf16[512,512]{1,0:T(8,128)(2,1)S(1)}, u32[]{:S(2)}, u32[]{:S(2)}) collective-permute-start(bf16[512,512]{1,0:T(8,128)(2,1)S(1)} %get-tuple-element.74.refs_0_), channel_id=1, source_target_pairs={{0,8},{2,10},{4,12},{6,14},{8,0},{10,2},{12,4},{14,6},{1,9},{3,11}... | collective-permute-start | bytes 1572872 | tf_op jit(solution)/shard_map/ppermute | solution.py:115
  117.5 26.4 %collective-permute-start.16 = (bf16[2,512,512]{2,1,0:T(8,128)(2,1)}, bf16[2,512,512]{2,1,0:T(8,128)(2,1)}, u32[]{:S(2)}, u32[]{:S(2)}) collective-permute-start(bf16[2,512,512]{2,1,0:T(8,128)(2,1)} %collective-permute-done.12.refs_9_.refs_3_), channel_id=1, source_target_pairs={{0,1},{1,0},{2,3},{3,2},{4,5},{5,4},{6,7},{7,6},{8,9},{9,8},{10,11... | collective-permute-start | bytes 3145736 | tf_op jit(solution)/shard_map/ppermute | solution.py:115
  125.2 53.4 %collective-permute-start.17 = (bf16[2,512,512]{2,1,0:T(8,128)(2,1)}, bf16[2,512,512]{2,1,0:T(8,128)(2,1)}, u32[]{:S(2)}, u32[]{:S(2)}) collective-permute-start(bf16[2,512,512]{2,1,0:T(8,128)(2,1)} %collective-permute-done.14.refs_11_.refs_5_), channel_id=1, source_target_pairs={{0,1},{1,0},{2,3},{3,2},{4,5},{5,4},{6,7},{7,6},{8,9},{9,8},{10,11... | collective-permute-start | bytes 3145736 | tf_op jit(solution)/shard_map/ppermute | solution.py:115
  141.0 25.0 %collective-permute-start.20 = (bf16[512,512]{1,0:T(8,128)(2,1)}, bf16[512,512]{1,0:T(8,128)(2,1)}, u32[]{:S(2)}, u32[]{:S(2)}) collective-permute-start(bf16[512,512]{1,0:T(8,128)(2,1)} %collective-permute-done.19.refs_2_), channel_id=1, source_target_pairs={{0,2},{2,0},{4,6},{6,4},{8,10},{10,8},{12,14},{14,12},{1,3},{3,1},... | collective-permute-start | bytes 1572872 | tf_op jit(solution)/shard_map/ppermute | solution.py:115
  142.3 34.9 %collective-permute-start.22 = (bf16[512,512]{1,0:T(8,128)(2,1)}, bf16[512,512]{1,0:T(8,128)(2,1)}, u32[]{:S(2)}, u32[]{:S(2)}) collective-permute-start(bf16[512,512]{1,0:T(8,128)(2,1)} %collective-permute-done.21.refs_4_), channel_id=1, source_target_pairs={{0,2},{2,0},{4,6},{6,4},{8,10},{10,8},{12,14},{14,12},{1,3},{3,1},... | collective-permute-start | bytes 1572872 | tf_op jit(solution)/shard_map/ppermute | solution.py:115
  143.9 50.9 %collective-permute-start.35 = (bf16[512,512]{1,0:T(8,128)(2,1)}, bf16[512,512]{1,0:T(8,128)(2,1)}, u32[]{:S(2)}, u32[]{:S(2)}) collective-permute-start(bf16[512,512]{1,0:T(8,128)(2,1)} %get-tuple-element.75), channel_id=1, source_target_pairs={{0,12},{2,14},{4,0},{6,2},{8,4},{10,6},{12,8},{14,10},{1,13},{3,15... | collective-permute-start | bytes 1572872 | tf_op jit(solution)/shard_map/ppermute | solution.py:115
  154.7 40.1 %collective-permute-start.2 = (bf16[512,512]{1,0:T(8,128)(2,1)S(1)}, bf16[512,512]{1,0:T(8,128)(2,1)}, u32[]{:S(2)}, u32[]{:S(2)}) collective-permute-start(bf16[512,512]{1,0:T(8,128)(2,1)S(1)} %get-tuple-element.74.refs_0_), channel_id=1, source_target_pairs={{0,2},{2,0},{4,6},{6,4},{8,10},{10,8},{12,14},{14,12},{1,3},{3,1},... | collective-permute-start | bytes 1572872 | tf_op jit(solution)/shard_map/ppermute | solution.py:115
  166.0 27.4 %collective-permute-start.7 = (bf16[512,512]{1,0:T(8,128)(2,1)}, bf16[512,512]{1,0:T(8,128)(2,1)}, u32[]{:S(2)}, u32[]{:S(2)}) collective-permute-start(bf16[512,512]{1,0:T(8,128)(2,1)} %copy-done.66), channel_id=1, source_target_pairs={{0,12},{2,14},{4,0},{6,2},{8,4},{10,6},{12,8},{14,10},{1,13},{3,15... | collective-permute-start | bytes 1572872 | tf_op jit(solution)/shard_map/ppermute | solution.py:115
  178.6 32.2 %collective-permute-start.6 = (bf16[512,512]{1,0:T(8,128)(2,1)}, bf16[512,512]{1,0:T(8,128)(2,1)S(1)}, u32[]{:S(2)}, u32[]{:S(2)}) collective-permute-start(bf16[512,512]{1,0:T(8,128)(2,1)} %collective-permute-done.5.refs_4_), channel_id=1, source_target_pairs={{0,2},{2,0},{4,6},{6,4},{8,10},{10,8},{12,14},{14,12},{1,3},{3,1},... | collective-permute-start | bytes 1572872 | tf_op jit(solution)/shard_map/ppermute | solution.py:115
  193.4 26.7 %collective-permute-start.8 = (bf16[512,512]{1,0:T(8,128)(2,1)}, bf16[512,512]{1,0:T(8,128)(2,1)S(1)}, u32[]{:S(2)}, u32[]{:S(2)}) collective-permute-start(bf16[512,512]{1,0:T(8,128)(2,1)} %collective-permute-done.7.refs_6_), channel_id=1, source_target_pairs={{0,2},{2,0},{4,6},{6,4},{8,10},{10,8},{12,14},{14,12},{1,3},{3,1},... | collective-permute-start | bytes 1572872 | tf_op jit(solution)/shard_map/ppermute | solution.py:115
  194.8 26.0 %collective-permute-start.23 = (bf16[512,512]{1,0:T(8,128)(2,1)S(1)}, bf16[512,512]{1,0:T(8,128)(2,1)S(1)}, u32[]{:S(2)}, u32[]{:S(2)}) collective-permute-start(bf16[512,512]{1,0:T(8,128)(2,1)S(1)} %get-tuple-element.43.refs_8_), channel_id=1, source_target_pairs={{0,4},{2,6},{4,0},{6,2},{8,12},{10,14},{12,8},{14,10},{1,5},{3,7},... | collective-permute-start | bytes 1572872 | tf_op jit(solution)/shard_map/ppermute | solution.py:115
  194.8 28.4 %collective-permute-start.37 = (bf16[512,512]{1,0:T(8,128)(2,1)S(1)}, bf16[512,512]{1,0:T(8,128)(2,1)S(1)}, u32[]{:S(2)}, u32[]{:S(2)}) collective-permute-start(bf16[512,512]{1,0:T(8,128)(2,1)S(1)} %get-tuple-element.44.refs_8_), channel_id=1, source_target_pairs={{0,4},{2,6},{4,0},{6,2},{8,12},{10,14},{12,8},{14,10},{1,5},{3,7},... | collective-permute-start | bytes 1572872 | tf_op jit(solution)/shard_map/ppermute | solution.py:115
  224.5 33.3 %collective-permute-start.26 = (bf16[512,512]{1,0:T(8,128)(2,1)S(1)}, bf16[512,512]{1,0:T(8,128)(2,1)}, u32[]{:S(2)}, u32[]{:S(2)}) collective-permute-start(bf16[512,512]{1,0:T(8,128)(2,1)S(1)} %collective-permute-done.23.refs_9_), channel_id=1, source_target_pairs={{0,16},{16,0},{1,17},{17,1},{2,18},{18,2},{3,19},{19,3},{4,20},{20... | collective-permute-start | bytes 1572872 | tf_op jit(solution)/shard_map/ppermute | solution.py:115
  227.6 30.1 %collective-permute-start.41 = (bf16[512,512]{1,0:T(8,128)(2,1)S(1)}, bf16[512,512]{1,0:T(8,128)(2,1)S(1)}, u32[]{:S(2)}, u32[]{:S(2)}) collective-permute-start(bf16[512,512]{1,0:T(8,128)(2,1)S(1)} %collective-permute-done.38.refs_10_), channel_id=1, source_target_pairs={{0,1},{1,0},{2,3},{3,2},{4,5},{5,4},{6,7},{7,6},{8,9},{9,8},{10,11... | collective-permute-start | bytes 1572872 | tf_op jit(solution)/shard_map/ppermute | solution.py:115
  248.5 33.5 %collective-permute-start.28 = (bf16[512,512]{1,0:T(8,128)(2,1)}, bf16[512,512]{1,0:T(8,128)(2,1)}, u32[]{:S(2)}, u32[]{:S(2)}) collective-permute-start(bf16[512,512]{1,0:T(8,128)(2,1)} %collective-permute-done.24.refs_10_), channel_id=1, source_target_pairs={{0,1},{1,0},{2,3},{3,2},{4,5},{5,4},{6,7},{7,6},{8,9},{9,8},{10,11... | collective-permute-start | bytes 1572872 | tf_op jit(solution)/shard_map/ppermute | solution.py:115
  258.6 37.5 %collective-permute-start.30 = (bf16[512,512]{1,0:T(8,128)(2,1)S(1)}, bf16[512,512]{1,0:T(8,128)(2,1)}, u32[]{:S(2)}, u32[]{:S(2)}) collective-permute-start(bf16[512,512]{1,0:T(8,128)(2,1)S(1)} %get-tuple-element.76.refs_0_), channel_id=1, source_target_pairs={{0,2},{2,0},{4,6},{6,4},{8,10},{10,8},{12,14},{14,12},{1,3},{3,1},... | collective-permute-start | bytes 1572872 | tf_op jit(solution)/shard_map/ppermute | solution.py:115
  260.9 36.7 %collective-permute-start.32 = (bf16[512,512]{1,0:T(8,128)(2,1)S(1)}, bf16[512,512]{1,0:T(8,128)(2,1)}, u32[]{:S(2)}, u32[]{:S(2)}) collective-permute-start(bf16[512,512]{1,0:T(8,128)(2,1)S(1)} %collective-permute-done.31.refs_2_), channel_id=1, source_target_pairs={{0,2},{2,0},{4,6},{6,4},{8,10},{10,8},{12,14},{14,12},{1,3},{3,1},... | collective-permute-start | bytes 1572872 | tf_op jit(solution)/shard_map/ppermute | solution.py:115
  262.3 35.4 %collective-permute-start.34 = (bf16[512,512]{1,0:T(8,128)(2,1)S(1)}, bf16[512,512]{1,0:T(8,128)(2,1)}, u32[]{:S(2)}, u32[]{:S(2)}) collective-permute-start(bf16[512,512]{1,0:T(8,128)(2,1)S(1)} %collective-permute-done.33.refs_4_), channel_id=1, source_target_pairs={{0,2},{2,0},{4,6},{6,4},{8,10},{10,8},{12,14},{14,12},{1,3},{3,1},... | collective-permute-start | bytes 1572872 | tf_op jit(solution)/shard_map/ppermute | solution.py:115
  282.1 24.5 %collective-permute-start.36 = (bf16[512,512]{1,0:T(8,128)(2,1)}, bf16[512,512]{1,0:T(8,128)(2,1)S(1)}, u32[]{:S(2)}, u32[]{:S(2)}) collective-permute-start(bf16[512,512]{1,0:T(8,128)(2,1)} %collective-permute-done.35.refs_6_), channel_id=1, source_target_pairs={{0,2},{2,0},{4,6},{6,4},{8,10},{10,8},{12,14},{14,12},{1,3},{3,1},... | collective-permute-start | bytes 1572872 | tf_op jit(solution)/shard_map/ppermute | solution.py:115
  307.5 26.0 %collective-permute-start.54 = (bf16[512,512]{1,0:T(8,128)(2,1)S(1)}, bf16[512,512]{1,0:T(8,128)(2,1)}, u32[]{:S(2)}, u32[]{:S(2)}) collective-permute-start(bf16[512,512]{1,0:T(8,128)(2,1)S(1)} %shard_map.19.refs_8_), channel_id=1, source_target_pairs={{0,16},{16,0},{1,17},{17,1},{2,18},{18,2},{3,19},{19,3},{4,20},{20... | collective-permute-start | bytes 1572872 | tf_op jit(solution)/shard_map/ppermute | solution.py:115
  313.1 30.1 %collective-permute-start.55 = (bf16[512,512]{1,0:T(8,128)(2,1)}, bf16[512,512]{1,0:T(8,128)(2,1)}, u32[]{:S(2)}, u32[]{:S(2)}) collective-permute-start(bf16[512,512]{1,0:T(8,128)(2,1)} %collective-permute-done.52.refs_9_), channel_id=1, source_target_pairs={{0,16},{16,0},{1,17},{17,1},{2,18},{18,2},{3,19},{19,3},{4,20},{20... | collective-permute-start | bytes 1572872 | tf_op jit(solution)/shard_map/ppermute | solution.py:115
  (99 other events, 916.2 us)

commit v3 on v2

--- a/solution.py
+++ b/solution.py
@@ -30,12 +30,12 @@
     return lax.optimization_barrier((value, *others))[0]
 
 
-def product_kernel(n_left, n_right, by_half, earlier, scale, place, *refs):
+def product_kernel(n_left, n_right, by_half, earlier, scale, form, place, *refs):
     left, refs = refs[:n_left], refs[n_left:]
     right, refs = refs[:n_right], refs[n_right:]
     before, refs = refs[:earlier], refs[earlier:]
     *outs, lscr, rscr, acc, lsem, rsem, asem = refs
-    halves, _, subs, cores, _, _ = rscr.shape
+    halves, _, subs, cores, _, w = rscr.shape
 
     def right_copy(i):
         y, s, c = place[1, i], place[2, i], place[3, i]
@@ -66,24 +66,41 @@
                 term += acc[h]
             if i < n_left - 1:
                 acc[h] = term
+            elif form == "sum":
+                outs[h][...] = term
             else:
-                outs[h][...] = (term * scale).astype(outs[h].dtype)
-
-
-def product(left, right, before, by_half, scale, segs, place, final):
+                term = (term * scale).astype(jnp.bfloat16).astype(jnp.float32)
+                low, high = term[:, : w // 2], term[:, w // 2 :]
+                if form == "ends":
+                    low, high = jnp.where(place[5, 0] == 0, low, high), jnp.where(place[5, 0] == 0, high, low)
+                if by_half:
+                    for out, value in zip(outs, (low, high)):
+                        out[:, h * w // 2 : (h + 1) * w // 2] = value.astype(out.dtype)
+                elif form == "ends":
+                    for out, value in zip(outs, (low, high)):
+                        out[...] = value.astype(out.dtype)
+                else:
+                    outs[0][...] = term.astype(outs[0].dtype)
+
+
+def product(left, right, before, by_half, scale, segs, place, form):
     q, w = left[0].shape
     n_left, n_right = len(left), len(right)
     halves = 2 if by_half else 1
+    if form == "ends":
+        shapes = [jax.ShapeDtypeStruct((q, w // 2), jnp.bfloat16)] * 2
+    else:
+        shapes = [jax.ShapeDtypeStruct((q, w), jnp.float32 if form == "sum" else jnp.bfloat16)] * halves
 
     def body(place_ref, *refs):
-        product_kernel(n_left, n_right, by_half, len(before), scale, place_ref, *refs)
+        product_kernel(n_left, n_right, by_half, len(before), scale, form, place_ref, *refs)
 
     return pl.pallas_call(
         body,
-        out_shape=[jax.ShapeDtypeStruct((q, w), jnp.bfloat16 if final else jnp.float32)] * halves,
+        out_shape=shapes,
         in_specs=[pl.BlockSpec(memory_space=pltpu.SMEM)]
         + [pl.BlockSpec(memory_space=pl.ANY)] * (n_left + n_right + len(before)),
-        out_specs=[pl.BlockSpec(memory_space=pltpu.VMEM)] * halves,
+        out_specs=[pl.BlockSpec(memory_space=pltpu.VMEM)] * len(shapes),
         scratch_shapes=[
             pltpu.VMEM((n_left, q, w), jnp.bfloat16),
             pltpu.VMEM((halves, segs, 2, 2, q, w), jnp.bfloat16),
@@ -99,6 +116,103 @@
     )(place, *left, *right, *before)
 
 
+def base_kernel(factor, place, own, *refs):
+    early, late, near, far = refs[:8], refs[8:16], refs[16:20], refs[20:22]
+    out, buf, sems, out_sems = refs[22:]
+    half = buf.shape[-1] // 2
+    c, zl = place[0], 1 - place[1]
+
+    def gathered(pieces, slot):
+        return [
+            pltpu.make_async_copy(
+                piece.at[:, pl.ds(pl.multiple_of(zl * half, half), half)],
+                buf.at[slot, zl ^ (i // 2 % 2), c ^ (i % 2), :, pl.ds(i // 4 * half, half)],
+                sems.at[i],
+            )
+            for i, piece in enumerate(pieces)
+        ]
+
+    def scale(slot):
+        for s in range(2):
+            for k in range(2):
+                buf[slot, s, k] = (buf[slot, s, k].astype(jnp.float32) * factor).astype(buf.dtype)
+
+    def run(first, second, scale_second):
+        for load in first + second:
+            load.start()
+        stores = [pltpu.make_async_copy(buf.at[slot], out.at[slot], out_sems.at[slot]) for slot in range(2)]
+        for slot, loads in enumerate((first, second)):
+            for load in loads:
+                load.wait()
+            if slot == 0 or scale_second:
+                scale(slot)
+            stores[slot].start()
+        for store in stores:
+            store.wait()
+
+    @pl.when(c == 0)
+    def _():
+        run([pltpu.make_async_copy(own, buf.at[0], sems.at[8])], gathered(early, 1), True)
+
+    @pl.when(c == 1)
+    def _():
+        ends = [(zl, i % 2, i // 2, piece) for i, piece in enumerate(near)]
+        ends += [(1 - zl, k, h, piece) for k, piece in enumerate(far) for h in range(2)]
+        copies = [
+            pltpu.make_async_copy(piece, buf.at[1, s, k, :, pl.ds(h * half, half)], sems.at[8 + i])
+            for i, (s, k, h, piece) in enumerate(ends)
+        ]
+        run(gathered(late, 0), copies, False)
+
+
+def assemble(factor, place, own, pieces):
+    spec = pl.BlockSpec(memory_space=pl.ANY)
+    return pl.pallas_call(
+        functools.partial(base_kernel, factor),
+        out_shape=jax.ShapeDtypeStruct((2, *own.shape), own.dtype),
+        in_specs=[pl.BlockSpec(memory_space=pltpu.SMEM)] + [spec] * (1 + len(pieces)),
+        out_specs=spec,
+        scratch_shapes=[
+            pltpu.VMEM((2, *own.shape), own.dtype),
+            pltpu.SemaphoreType.DMA((16,)),
+            pltpu.SemaphoreType.DMA((2,)),
+        ],
+        compiler_params=pltpu.CompilerParams(vmem_limit_bytes=24 << 20),
+    )(place, own, *pieces)
+
+
+def finish_kernel(place, base, first, second, out, scr, sems):
+    _, half = first.shape
+
+    @pl.when(place[0] == 1)
+    def _():
+        pieces = (first, second)
+        loads = [pltpu.make_async_copy(p, scr.at[k], sems.at[0, k]) for k, p in enumerate(pieces)]
+        stores = [
+            pltpu.make_async_copy(scr.at[k], out.at[1, place[1], k, :, pl.ds(half, half)], sems.at[1, k])
+            for k in range(2)
+        ]
+        for load in loads:
+            load.start()
+        for load, store in zip(loads, stores):
+            load.wait()
+            store.start()
+        for store in stores:
+            store.wait()
+
+
+def finish(place, base, pieces):
+    spec = pl.BlockSpec(memory_space=pl.ANY)
+    return pl.pallas_call(
+        finish_kernel,
+        out_shape=jax.ShapeDtypeStruct(base.shape, base.dtype),
+        in_specs=[pl.BlockSpec(memory_space=pltpu.SMEM)] + [spec] * 3,
+        out_specs=spec,
+        scratch_shapes=[pltpu.VMEM((2, *pieces[0].shape), base.dtype), pltpu.SemaphoreType.DMA((2, 2))],
+        input_output_aliases={1: 0},
+    )(place, base, *pieces)
+
+
 def local(fast, slices):
     segs, rows, _ = (lax.axis_size(a) for a in ("seg", "row", "col"))
     slow = rows // fast
@@ -182,14 +296,14 @@
             for dy in range(1, segs) if others else [0]:
                 self.add((dy, s, 1), core_swap(self.block(dy, s, 0)))
 
-    def part(left, chosen, right, before, by_half, scale, final):
+    def part(left, chosen, right, before, by_half, scale, form):
         places = [left.places()[i] for i in chosen]
         table = [places] + right.places()
         flags = []
         for ry, rs, rc in zip(*table[1:]):
             match = lambda k: (k // 4 == ry) & (k % 2 == rc) & (by_half | (k // 2 % 2 == rs))
             flags.append(functools.reduce(jnp.logical_or, [match(k) for k in places]))
-        table.append(flags)
+        table += [flags, [zl]]
         width = max(len(t) for t in table)
         zero = jnp.int32(0)
         place = jnp.stack(
@@ -203,12 +317,15 @@
             scale,
             segs,
             place,
-            final,
+            form,
         )
 
     def own_block(halves):
+        def columns(block):
+            return jnp.where(zl == 0, block[:, : w // 2], block[:, w // 2 :])
+
         found = {
-            (t, k): jnp.where(zl == 0, *(right.block(0, t, k) for right in halves))
+            (t, k): jnp.concatenate([columns(right.block(0, t, k)) for right in halves], axis=1)
             for t in range(2)
             for k in range(2)
         }
@@ -251,9 +368,9 @@
     left.over_fast(coming[-1])
     rest += 1
     right.cross(1, others=True)
-    ready = part(left, range(rest), right, [], True, 1.0, fast == 1)
+    ready = part(left, range(rest), right, [], True, 1.0, "sum" if fast > 1 else "whole")
     if fast > 1:
-        ready = part(left, range(rest, len(left.pieces)), right, ready, True, 1.0, True)
+        ready = part(left, range(rest, len(left.pieces)), right, ready, True, 1.0, "whole")
 
     a, b = Right(ready[0]), Right(ready[1])
     plane = a.plane()
@@ -268,10 +385,10 @@
     a.cross(1)
     a.cross(0, others=True)
     left2.over_fast(early[-1])
-    early3 = [left3.over_slow(j) for j in (*evens, *odds)]
+    early3 = [left3.over_slow(j) for j in (*odds, *evens)]
     b.segs(1)
     a.cross(1, others=True)
-    (ready_a,) = part(left2, range(len(left2.pieces)), a, [], False, 1.0, True)
+    (ready_a,) = part(left2, range(len(left2.pieces)), a, [], False, 1.0, "whole")
     a3 = Right(ready_a)
     a3.plane()
     a3.segs(0)
@@ -280,7 +397,7 @@
     b.cross(1)
     left3.over_fast(early3[0])
     b.cross(1, others=True)
-    (ready_b,) = part(left2, range(len(left2.pieces)), b, [], False, 1.0, True)
+    (ready_b,) = part(left2, range(len(left2.pieces)), b, [], False, 1.0, "whole")
     b3 = Right(ready_b)
 
     b3.plane()
@@ -293,33 +410,33 @@
     a3.cross(0, others=True)
     b3.segs(1)
     a3.cross(1, others=True)
-    (last_a,) = part(left3, range(len(left3.pieces)), a3, [], False, factor, True)
-
-    def home(h, value):
-        slots = [i * 2 + k for i in range(rows) for k in range(2) if (i // fast) % 2 != h]
-        moved = [
-            send(value, ("row", "col"), [(i, partner(i // 2) * 2 + 1) for i in slots if i % 2 == k])
-            for k in range(2)
-        ]
-        slots = [i for i in range(rows) if (i // fast) % 2 == h]
-        kept = send(value, ("row", "col"), [(i * 2, i * 2 + 1) for i in slots])
-        return kept, moved
-
-    kept_a, moved_a = home(0, last_a)
+    last_a = part(left3, range(len(left3.pieces)), a3, [], False, factor, "ends")
+
+    def home(keep, away):
+        moved = [send(away, ("row", "col"), [(i * 2 + k, partner(i) * 2 + 1) for i in range(rows)]) for k in range(2)]
+        return [send(keep, "col", [(0, 1)]), keep], moved
+
+    here_a, far_a = home(*last_a)
     b3.cross(1)
     b3.cross(0, others=True)
     b3.cross(1, others=True)
-    (last_b,) = part(left3, range(len(left3.pieces)), b3, [], False, factor, True)
-    kept_b, moved_b = home(1, last_b)
-    here = jnp.where(zl == 0, jnp.stack([kept_a, last_a]), jnp.stack([kept_b, last_b]))
-    there = jnp.where(zl == 0, jnp.stack(moved_a), jnp.stack(moved_b))
+    last_b = part(left3, range(len(left3.pieces)), b3, [], False, factor, "ends")
+    here_b, far_b = home(*last_b)
+    if w % 512 == 0:
+        place = jnp.stack([c, 1 - zl]).astype(jnp.int32)
+        keys = [(t, k) for t in range(2) for k in range(2)]
+        pieces = [right.block(0, *key) for halves in ((a, b), (a3, b3)) for right in halves for key in keys]
+        base = assemble(factor, place, parts[0], [*pieces, *here_a, *here_b, *far_a])
+        return finish(place, base, far_b).reshape(2, height, w)
+    here = jnp.stack([jnp.concatenate([here_a[k], here_b[k]], axis=1) for k in range(2)])
+    there = jnp.stack([jnp.concatenate([far_a[k], far_b[k]], axis=1) for k in range(2)])
     final = jnp.stack([jnp.where(zl == s, here, there) for s in range(2)])
 
     def scaled(value):
         return (value.astype(jnp.float32) * factor).astype(jnp.bfloat16)
 
     for item in (a, b, a3, b3):
-        item.pieces = [(*p[:3], after(p[3], last_b)) for p in item.pieces]
+        item.pieces = [(*p[:3], after(p[3], last_b[0])) for p in item.pieces]
     head = jnp.where(c == 0, slices[0].reshape(2, 2, q, w), own_block((a3, b3)))
     tail = jnp.where(c == 0, scaled(own_block((a, b))), final)
     return jnp.stack([scaled(head).reshape(height, w), tail.reshape(height, w)], axis=0)

time: 384 us -> 373 us (0.971)
  waiting for transfers between devices: 196 us -> 148 us
  starting transfers between devices: 82.9 us -> 119 us
  Pallas kernels: 30.5 us -> 35.4 us
  other arithmetic: 14.5 us -> 9.82 us
    ppermute x64, waiting for transfers between devices: 196 us -> 148 us  [send(): return lax.ppermute(value, axes, pairs)]
    ppermute x64, starting transfers between devices: 82.9 us -> 119 us  [send(): return lax.ppermute(value, axes, pairs)]
    another operation x11 -> x1, other arithmetic: 5.14 us -> 0.07 us  [local(): place = jnp.stack([c, 1 - zl]).astype(jnp.int32)]
    pallas_call x6 -> x8, Pallas kernels: 30.5 us -> 35.4 us  [the longest x6 31.3 us: product(): pl.pallas_call(body, out_shape=shapes, in_specs=[pl.BlockSpec(memory_spac...]
    unnamed x134 -> x138, local copies, waits for them, and re-layouts: 47.3 us -> 47.9 us
  transfers between devices with their start and end apart: 64 -> 64, of which waited for: 21 -> 17; matrix products, arithmetic and copies ran while one was open for 3% -> 3% of each run, Pallas kernels for 8% -> 9%
where the time goes in v3:
time: 373 us; the launch traced here: 368 us
  waiting for transfers between devices  148 us (40%)
  starting transfers between devices  119 us (32%)
  local copies, waits for them, and re-layouts  54.1 us (15%)
  Pallas kernels  35.4 us (9%)
  other arithmetic  9.82 us (3%)
    ppermute x64, waiting for transfers between devices, send(): return lax.ppermute(value, axes, pairs)  148 us
    ppermute x64, starting transfers between devices, send(): return lax.ppermute(value, axes, pairs)  119 us
    unnamed x138, local copies, waits for them, and re-layouts  47.9 us
    pallas_call x6, Pallas kernels, product(): pl.pallas_call(body, out_shape=shapes, in_specs=[pl.BlockSpec(memory_spac...  31.3 us
  transfers between devices with their start and end apart: 64, of which 17 were waited for; matrix products, arithmetic and copies ran while one was open for 3% of the time, Pallas kernels for 9%

profile of v3, /device:TPU:0, one launch (start us, length us, event | category | flops | bytes accessed | tf_op | source)
XLA Modules:
  0.0 368.1 jit_solution(626632397295523050)
XLA Ops:
  8.8 2.9 collective-permute-start.4
  14.9 3.3 collective-permute-start.2
  19.7 16.4 %collective-permute-done.4.refs_8_.refs_2_ = bf16[2,512,512]{2,1,0:T(8,128)(2,1)} collective-permute-done((bf16[2,512,512]{2,1,0:T(8,128)(2,1)}, bf16[2,512,512]{2,1,0:T(8,128)(2,1)}, u32[]{:S(2)}, u32[]{:S(2)}) %collective-permute-start.4) | collective-permute-done | bytes 1048608 | tf_op jit(solution)/shard_map/ppermute | solution.py:229
  36.1 3.0 collective-permute-start.12
  43.3 11.7 %collective-permute-start.14 = (bf16[512,512]{1,0:T(8,128)(2,1)S(1)}, bf16[512,512]{1,0:T(8,128)(2,1)S(1)}, u32[]{:S(2)}, u32[]{:S(2)}) collective-permute-start(bf16[512,512]{1,0:T(8,128)(2,1)S(1)} %get-tuple-element.36), channel_id=1, source_target_pairs={{0,4},{2,6},{4,8},{6,10},{8,12},{10,14},{12,0},{14,2},{1,5},{3,7},... | collective-permute-start | bytes 1572872 | tf_op jit(solution)/shard_map/ppermute | solution.py:229
  59.7 24.9 %collective-permute-done.12.refs_2_ = bf16[512,512]{1,0:T(8,128)(2,1)} collective-permute-done((bf16[512,512]{1,0:T(8,128)(2,1)S(1)}, bf16[512,512]{1,0:T(8,128)(2,1)}, u32[]{:S(2)}, u32[]{:S(2)}) %collective-permute-start.12) | collective-permute-done | bytes 524320 | tf_op jit(solution)/shard_map/ppermute | solution.py:229
  85.9 7.4 %collective-permute-start.25 = (bf16[512,512]{1,0:T(8,128)(2,1)S(1)}, bf16[512,512]{1,0:T(8,128)(2,1)}, u32[]{:S(2)}, u32[]{:S(2)}) collective-permute-start(bf16[512,512]{1,0:T(8,128)(2,1)S(1)} %get-tuple-element.33), channel_id=1, source_target_pairs={{0,4},{2,6},{4,8},{6,10},{8,12},{10,14},{12,0},{14,2},{1,5},{3,7},... | collective-permute-start | bytes 1572872 | tf_op jit(solution)/shard_map/ppermute | solution.py:229
  93.4 13.0 %collective-permute-done.23.refs_2_ = bf16[512,512]{1,0:T(8,128)(2,1)S(1)} collective-permute-done((bf16[512,512]{1,0:T(8,128)(2,1)S(1)}, bf16[512,512]{1,0:T(8,128)(2,1)S(1)}, u32[]{:S(2)}, u32[]{:S(2)}) %collective-permute-start.23) | collective-permute-done | bytes 524320 | tf_op jit(solution)/shard_map/ppermute | solution.py:229
  108.2 11.0 %collective-permute-done.27.refs_6_ = bf16[512,512]{1,0:T(8,128)(2,1)} collective-permute-done((bf16[512,512]{1,0:T(8,128)(2,1)S(1)}, bf16[512,512]{1,0:T(8,128)(2,1)}, u32[]{:S(2)}, u32[]{:S(2)}) %collective-permute-start.27) | collective-permute-done | bytes 524320 | tf_op jit(solution)/shard_map/ppermute | solution.py:229
  124.3 8.4 %collective-permute-start.44 = (bf16[512,512]{1,0:T(8,128)(2,1)}, bf16[512,512]{1,0:T(8,128)(2,1)}, u32[]{:S(2)}, u32[]{:S(2)}) collective-permute-start(bf16[512,512]{1,0:T(8,128)(2,1)} %get-tuple-element.31), channel_id=1, source_target_pairs={{0,4},{2,6},{4,8},{6,10},{8,12},{10,14},{12,0},{14,2},{1,5},{3,7},... | collective-permute-start | bytes 1572872 | tf_op jit(solution)/shard_map/ppermute | solution.py:229
  132.8 11.4 %collective-permute-start.46 = (bf16[512,512]{1,0:T(8,128)(2,1)}, bf16[512,512]{1,0:T(8,128)(2,1)}, u32[]{:S(2)}, u32[]{:S(2)}) collective-permute-start(bf16[512,512]{1,0:T(8,128)(2,1)} %get-tuple-element.31), channel_id=1, source_target_pairs={{0,12},{2,14},{4,0},{6,2},{8,4},{10,6},{12,8},{14,10},{1,13},{3,15... | collective-permute-start | bytes 1572872 | tf_op jit(solution)/shard_map/ppermute | solution.py:229
  144.2 10.4 %collective-permute-start.48 = (bf16[512,512]{1,0:T(8,128)(2,1)}, bf16[512,512]{1,0:T(8,128)(2,1)}, u32[]{:S(2)}, u32[]{:S(2)}) collective-permute-start(bf16[512,512]{1,0:T(8,128)(2,1)} %get-tuple-element.32.refs_0_), channel_id=1, source_target_pairs={{0,8},{2,10},{4,12},{6,14},{8,0},{10,2},{12,4},{14,6},{1,9},{3,11}... | collective-permute-start | bytes 1572872 | tf_op jit(solution)/shard_map/ppermute | solution.py:229
  159.8 8.4 %shard_map.17 = (f32[512,512]{1,0:T(8,128)S(1)}, f32[512,512]{1,0:T(8,128)S(1)}) custom-call(s32[6,8]{1,0:T(8,128)S(1)} %stack.245.place_ref, bf16[512,512]{1,0:T(8,128)(2,1)S(1)} %copy-done.55, bf16[512,512]{1,0:T(8,128)(2,1)S(1)} %copy-done.62, bf16[512,512]{1,0:T(8,128)(2,1)} %collective-permute-done.12.refs_2_, ...), custom_call_target="tpu_custom_call" | custom-call | flops 3758096384 | bytes 11010048 | tf_op jit(solution)/shard_map/pallas_call | solution.py:98
  168.3 3.1 shard_map.18
  173.0 8.1 %collective-permute-done.48.refs_6_ = bf16[512,512]{1,0:T(8,128)(2,1)} collective-permute-done((bf16[512,512]{1,0:T(8,128)(2,1)}, bf16[512,512]{1,0:T(8,128)(2,1)}, u32[]{:S(2)}, u32[]{:S(2)}) %collective-permute-start.48) | collective-permute-done | bytes 524320 | tf_op jit(solution)/shard_map/ppermute | solution.py:229
  183.0 6.7 %collective-permute-start.20 = (bf16[512,512]{1,0:T(8,128)(2,1)S(1)}, bf16[512,512]{1,0:T(8,128)(2,1)S(1)}, u32[]{:S(2)}, u32[]{:S(2)}) collective-permute-start(bf16[512,512]{1,0:T(8,128)(2,1)S(1)} %get-tuple-element.20.refs_8_.refs_4_), channel_id=1, source_target_pairs={{0,4},{2,6},{4,0},{6,2},{8,12},{10,14},{12,8},{14,10},{1,5},{3,7},... | collective-permute-start | bytes 1572872 | tf_op jit(solution)/shard_map/ppermute | solution.py:229
  199.0 7.2 %collective-permute-done.20.refs_9_.refs_6_ = bf16[512,512]{1,0:T(8,128)(2,1)S(1)} collective-permute-done((bf16[512,512]{1,0:T(8,128)(2,1)S(1)}, bf16[512,512]{1,0:T(8,128)(2,1)S(1)}, u32[]{:S(2)}, u32[]{:S(2)}) %collective-permute-start.20) | collective-permute-done | bytes 524320 | tf_op jit(solution)/shard_map/ppermute | solution.py:229
  208.4 8.2 %collective-permute-done.36.refs_10_ = bf16[512,512]{1,0:T(8,128)(2,1)} collective-permute-done((bf16[512,512]{1,0:T(8,128)(2,1)S(1)}, bf16[512,512]{1,0:T(8,128)(2,1)}, u32[]{:S(2)}, u32[]{:S(2)}) %collective-permute-start.36) | collective-permute-done | bytes 524320 | tf_op jit(solution)/shard_map/ppermute | solution.py:229
  217.4 10.3 %collective-permute-done.30.refs_12_ = bf16[512,512]{1,0:T(8,128)(2,1)S(1)} collective-permute-done((bf16[512,512]{1,0:T(8,128)(2,1)S(1)}, bf16[512,512]{1,0:T(8,128)(2,1)S(1)}, u32[]{:S(2)}, u32[]{:S(2)}) %collective-permute-start.30) | collective-permute-done | bytes 524320 | tf_op jit(solution)/shard_map/ppermute | solution.py:229
  229.9 4.5 %collective-permute-done.37.refs_12_ = bf16[512,512]{1,0:T(8,128)(2,1)} collective-permute-done((bf16[512,512]{1,0:T(8,128)(2,1)S(1)}, bf16[512,512]{1,0:T(8,128)(2,1)}, u32[]{:S(2)}, u32[]{:S(2)}) %collective-permute-start.37) | collective-permute-done | bytes 524320 | tf_op jit(solution)/shard_map/ppermute | solution.py:229
  254.9 4.0 %shard_map.19.refs_8_ = bf16[512,512]{1,0:T(8,128)(2,1)S(1)} custom-call(s32[6,8]{1,0:T(8,128)S(1)} %stack.266.place_ref, bf16[512,512]{1,0:T(8,128)(2,1)S(1)} %get-tuple-element.34.refs_0_, bf16[512,512]{1,0:T(8,128)(2,1)S(1)} %copy-done.1, bf16[512,512]{1,0:T(8,128)(2,1)S(1)} %copy-done.4, bf16[512,512]{1,0:T(8,128)(2,1)S(1)} %copy-done.31, ...), custom_call_target="tpu_custom_call" | custom-call | flops 2147483648 | bytes 8388608 | tf_op jit(solution)/shard_map/pallas_call | solution.py:98
  259.0 10.7 %collective-permute-start.34 = (bf16[512,512]{1,0:T(8,128)(2,1)S(1)}, bf16[512,512]{1,0:T(8,128)(2,1)}, u32[]{:S(2)}, u32[]{:S(2)}) collective-permute-start(bf16[512,512]{1,0:T(8,128)(2,1)S(1)} %shard_map.19.refs_8_), channel_id=1, source_target_pairs={{0,4},{2,6},{4,0},{6,2},{8,12},{10,14},{12,8},{14,10},{1,5},{3,7},... | collective-permute-start | bytes 1572872 | tf_op jit(solution)/shard_map/ppermute | solution.py:229
  279.9 4.9 %shard_map.20.refs_8_.refs_12_ = bf16[512,512]{1,0:T(8,128)(2,1)} custom-call(s32[6,8]{1,0:T(8,128)S(1)} %stack.273.place_ref, bf16[512,512]{1,0:T(8,128)(2,1)S(1)} %get-tuple-element.34.refs_0_, bf16[512,512]{1,0:T(8,128)(2,1)S(1)} %copy-done.2, bf16[512,512]{1,0:T(8,128)(2,1)S(1)} %copy-done.5, bf16[512,512]{1,0:T(8,128)(2,1)S(1)} %copy-done.32, ...), custom_call_target="tpu_custom_call" | custom-call | flops 2147483648 | bytes 8388608 | tf_op jit(solution)/shard_map/pallas_call | solution.py:98
  290.0 9.8 %collective-permute-done.50.refs_10_ = bf16[512,512]{1,0:T(8,128)(2,1)S(1)} collective-permute-done((bf16[512,512]{1,0:T(8,128)(2,1)S(1)}, bf16[512,512]{1,0:T(8,128)(2,1)S(1)}, u32[]{:S(2)}, u32[]{:S(2)}) %collective-permute-start.50) | collective-permute-done | bytes 524320 | tf_op jit(solution)/shard_map/ppermute | solution.py:229
  302.6 8.5 %collective-permute-done.51.refs_12_ = bf16[512,512]{1,0:T(8,128)(2,1)} collective-permute-done((bf16[512,512]{1,0:T(8,128)(2,1)}, bf16[512,512]{1,0:T(8,128)(2,1)}, u32[]{:S(2)}, u32[]{:S(2)}) %collective-permute-start.51) | collective-permute-done | bytes 524320 | tf_op jit(solution)/shard_map/ppermute | solution.py:229
  311.2 11.2 %collective-permute-done.55.refs_10_ = bf16[512,512]{1,0:T(8,128)(2,1)} collective-permute-done((bf16[512,512]{1,0:T(8,128)(2,1)}, bf16[512,512]{1,0:T(8,128)(2,1)}, u32[]{:S(2)}, u32[]{:S(2)}) %collective-permute-start.55) | collective-permute-done | bytes 524320 | tf_op jit(solution)/shard_map/ppermute | solution.py:229
  324.5 8.8 %collective-permute-done.56.refs_12_ = bf16[512,512]{1,0:T(8,128)(2,1)} collective-permute-done((bf16[512,512]{1,0:T(8,128)(2,1)}, bf16[512,512]{1,0:T(8,128)(2,1)}, u32[]{:S(2)}, u32[]{:S(2)}) %collective-permute-start.56) | collective-permute-done | bytes 524320 | tf_op jit(solution)/shard_map/ppermute | solution.py:229
  338.0 5.0 %shard_map.21 = (bf16[512,256]{1,0:T(8,128)(2,1)S(1)}, bf16[512,256]{1,0:T(8,128)(2,1)S(1)}) custom-call(s32[6,8]{1,0:T(8,128)S(1)} %stack.287.place_ref, bf16[512,512]{1,0:T(8,128)(2,1)} %get-tuple-element.32.refs_0_, bf16[512,512]{1,0:T(8,128)(2,1)} %collective-permute-done.43.refs_1_, bf16[512,512]{1,0:T(8,128)(2,1)} %collective-permute-done.44.refs_2_, ...), custom_call_target="tpu_custom_call" | custom-call | flops 2147483648 | bytes 8388608 | tf_op jit(solution)/shard_map/pallas_call | solution.py:98
  343.1 3.0 collective-permute-start.54
  346.2 5.7 %shard_map.22 = (bf16[512,256]{1,0:T(8,128)(2,1)S(1)}, bf16[512,256]{1,0:T(8,128)(2,1)S(1)}) custom-call(s32[6,8]{1,0:T(8,128)S(1)} %stack.287.place_ref, bf16[512,512]{1,0:T(8,128)(2,1)} %get-tuple-element.32.refs_0_, bf16[512,512]{1,0:T(8,128)(2,1)} %collective-permute-done.43.refs_1_, bf16[512,512]{1,0:T(8,128)(2,1)} %collective-permute-done.44.refs_2_, ...), custom_call_target="tpu_custom_call" | custom-call | flops 2147483648 | bytes 8388608 | tf_op jit(solution)/shard_map/pallas_call | solution.py:98
  355.5 3.9 %collective-permute-start.62 = (bf16[512,256]{1,0:T(8,128)(2,1)S(1)}, bf16[512,256]{1,0:T(8,128)(2,1)S(1)}, u32[]{:S(2)}, u32[]{:S(2)}) collective-permute-start(bf16[512,256]{1,0:T(8,128)(2,1)S(1)} %get-tuple-element.26), channel_id=1, source_target_pairs={{0,5},{2,7},{4,1},{6,3},{8,13},{10,15},{12,9},{14,11},{16,21},{18,... | collective-permute-start | bytes 786440 | tf_op jit(solution)/shard_map/ppermute | solution.py:229
  361.0 3.4 shard_map.23.base
  (276 shorter events, 106.8 us)
Async XLA Ops:
  8.8 27.3 %collective-permute-start.4 = (bf16[2,512,512]{2,1,0:T(8,128)(2,1)}, bf16[2,512,512]{2,1,0:T(8,128)(2,1)}, u32[]{:S(2)}, u32[]{:S(2)}) collective-permute-start(bf16[2,512,512]{2,1,0:T(8,128)(2,1)} %broadcast_select_fusion.1.refs_7_.refs_1_), channel_id=1, source_target_pairs={{0,4},{2,6},{4,0},{6,2},{8,12},{10,14},{12,8},{14,10},{1,5},{3,7},... | collective-permute-start | bytes 3145736 | tf_op jit(solution)/shard_map/ppermute | solution.py:229
  11.8 27.4 %collective-permute-start.5 = (bf16[2,512,512]{2,1,0:T(8,128)(2,1)}, bf16[2,512,512]{2,1,0:T(8,128)(2,1)}, u32[]{:S(2)}, u32[]{:S(2)}) collective-permute-start(bf16[2,512,512]{2,1,0:T(8,128)(2,1)} %broadcast_select_fusion.1.refs_7_.refs_1_), channel_id=1, source_target_pairs={{0,16},{16,0},{1,17},{17,1},{2,18},{18,2},{3,19},{19,3},{4,20},{20... | collective-permute-start | bytes 3145736 | tf_op jit(solution)/shard_map/ppermute | solution.py:229
  13.3 30.0 %collective-permute-start.6 = (bf16[2,512,512]{2,1,0:T(8,128)(2,1)}, bf16[2,512,512]{2,1,0:T(8,128)(2,1)}, u32[]{:S(2)}, u32[]{:S(2)}) collective-permute-start(bf16[2,512,512]{2,1,0:T(8,128)(2,1)} %broadcast_select_fusion.1.refs_7_.refs_1_), channel_id=1, source_target_pairs={{0,1},{1,0},{2,3},{3,2},{4,5},{5,4},{6,7},{7,6},{8,9},{9,8},{10,11... | collective-permute-start | bytes 3145736 | tf_op jit(solution)/shard_map/ppermute | solution.py:229
  14.9 42.2 %collective-permute-start.2 = (bf16[512,512]{1,0:T(8,128)(2,1)S(1)}, bf16[512,512]{1,0:T(8,128)(2,1)}, u32[]{:S(2)}, u32[]{:S(2)}) collective-permute-start(bf16[512,512]{1,0:T(8,128)(2,1)S(1)} %get-tuple-element.36), channel_id=1, source_target_pairs={{0,12},{2,14},{4,0},{6,2},{8,4},{10,6},{12,8},{14,10},{1,13},{3,15... | collective-permute-start | bytes 1572872 | tf_op jit(solution)/shard_map/ppermute | solution.py:229
  18.2 40.6 %collective-permute-start.11 = (bf16[512,512]{1,0:T(8,128)(2,1)S(1)}, bf16[512,512]{1,0:T(8,128)(2,1)S(1)}, u32[]{:S(2)}, u32[]{:S(2)}) collective-permute-start(bf16[512,512]{1,0:T(8,128)(2,1)S(1)} %get-tuple-element.35.refs_0_), channel_id=1, source_target_pairs={{0,2},{2,0},{4,6},{6,4},{8,10},{10,8},{12,14},{14,12},{1,3},{3,1},... | collective-permute-start | bytes 1572872 | tf_op jit(solution)/shard_map/ppermute | solution.py:229
  36.1 48.5 %collective-permute-start.12 = (bf16[512,512]{1,0:T(8,128)(2,1)S(1)}, bf16[512,512]{1,0:T(8,128)(2,1)}, u32[]{:S(2)}, u32[]{:S(2)}) collective-permute-start(bf16[512,512]{1,0:T(8,128)(2,1)S(1)} %get-tuple-element.35.refs_0_), channel_id=1, source_target_pairs={{0,8},{2,10},{4,12},{6,14},{8,0},{10,2},{12,4},{14,6},{1,9},{3,11}... | collective-permute-start | bytes 1572872 | tf_op jit(solution)/shard_map/ppermute | solution.py:229
  39.1 67.5 %collective-permute-start.7 = (bf16[2,512,512]{2,1,0:T(8,128)(2,1)}, bf16[2,512,512]{2,1,0:T(8,128)(2,1)}, u32[]{:S(2)}, u32[]{:S(2)}) collective-permute-start(bf16[2,512,512]{2,1,0:T(8,128)(2,1)} %collective-permute-done.4.refs_8_.refs_2_), channel_id=1, source_target_pairs={{0,16},{16,0},{1,17},{17,1},{2,18},{18,2},{3,19},{19,3},{4,20},{20... | collective-permute-start | bytes 3145736 | tf_op jit(solution)/shard_map/ppermute | solution.py:229
  43.3 41.3 %collective-permute-start.14 = (bf16[512,512]{1,0:T(8,128)(2,1)S(1)}, bf16[512,512]{1,0:T(8,128)(2,1)S(1)}, u32[]{:S(2)}, u32[]{:S(2)}) collective-permute-start(bf16[512,512]{1,0:T(8,128)(2,1)S(1)} %get-tuple-element.36), channel_id=1, source_target_pairs={{0,4},{2,6},{4,8},{6,10},{8,12},{10,14},{12,0},{14,2},{1,5},{3,7},... | collective-permute-start | bytes 1572872 | tf_op jit(solution)/shard_map/ppermute | solution.py:229
  57.1 28.0 %collective-permute-start.22 = (bf16[512,512]{1,0:T(8,128)(2,1)S(1)}, bf16[512,512]{1,0:T(8,128)(2,1)S(1)}, u32[]{:S(2)}, u32[]{:S(2)}) collective-permute-start(bf16[512,512]{1,0:T(8,128)(2,1)S(1)} %get-tuple-element.34.refs_0_), channel_id=1, source_target_pairs={{0,2},{2,0},{4,6},{6,4},{8,10},{10,8},{12,14},{14,12},{1,3},{3,1},... | collective-permute-start | bytes 1572872 | tf_op jit(solution)/shard_map/ppermute | solution.py:229
  59.7 46.7 %collective-permute-start.23 = (bf16[512,512]{1,0:T(8,128)(2,1)S(1)}, bf16[512,512]{1,0:T(8,128)(2,1)S(1)}, u32[]{:S(2)}, u32[]{:S(2)}) collective-permute-start(bf16[512,512]{1,0:T(8,128)(2,1)S(1)} %get-tuple-element.34.refs_0_), channel_id=1, source_target_pairs={{0,8},{2,10},{4,12},{6,14},{8,0},{10,2},{12,4},{14,6},{1,9},{3,11}... | collective-permute-start | bytes 1572872 | tf_op jit(solution)/shard_map/ppermute | solution.py:229
  84.6 36.2 %collective-permute-start.8 = (bf16[2,512,512]{2,1,0:T(8,128)(2,1)}, bf16[2,512,512]{2,1,0:T(8,128)(2,1)}, u32[]{:S(2)}, u32[]{:S(2)}) collective-permute-start(bf16[2,512,512]{2,1,0:T(8,128)(2,1)} %collective-permute-done.4.refs_8_.refs_2_), channel_id=1, source_target_pairs={{0,1},{1,0},{2,3},{3,2},{4,5},{5,4},{6,7},{7,6},{8,9},{9,8},{10,11... | collective-permute-start | bytes 3145736 | tf_op jit(solution)/shard_map/ppermute | solution.py:229
  84.6 39.7 %collective-permute-start.9 = (bf16[2,512,512]{2,1,0:T(8,128)(2,1)}, bf16[2,512,512]{2,1,0:T(8,128)(2,1)}, u32[]{:S(2)}, u32[]{:S(2)}) collective-permute-start(bf16[2,512,512]{2,1,0:T(8,128)(2,1)} %collective-permute-done.5.refs_9_.refs_3_), channel_id=1, source_target_pairs={{0,1},{1,0},{2,3},{3,2},{4,5},{5,4},{6,7},{7,6},{8,9},{9,8},{10,11... | collective-permute-start | bytes 3145736 | tf_op jit(solution)/shard_map/ppermute | solution.py:229
  106.6 49.5 %collective-permute-start.10 = (bf16[2,512,512]{2,1,0:T(8,128)(2,1)}, bf16[2,512,512]{2,1,0:T(8,128)(2,1)}, u32[]{:S(2)}, u32[]{:S(2)}) collective-permute-start(bf16[2,512,512]{2,1,0:T(8,128)(2,1)} %collective-permute-done.7.refs_11_.refs_5_), channel_id=1, source_target_pairs={{0,1},{1,0},{2,3},{3,2},{4,5},{5,4},{6,7},{7,6},{8,9},{9,8},{10,11... | collective-permute-start | bytes 3145736 | tf_op jit(solution)/shard_map/ppermute | solution.py:229
  106.7 26.1 %collective-permute-start.3 = (bf16[512,512]{1,0:T(8,128)(2,1)}, bf16[512,512]{1,0:T(8,128)(2,1)}, u32[]{:S(2)}, u32[]{:S(2)}) collective-permute-start(bf16[512,512]{1,0:T(8,128)(2,1)} %collective-permute-done.2.refs_6_), channel_id=1, source_target_pairs={{0,2},{2,0},{4,6},{6,4},{8,10},{10,8},{12,14},{14,12},{1,3},{3,1},... | collective-permute-start | bytes 1572872 | tf_op jit(solution)/shard_map/ppermute | solution.py:229
  120.8 33.8 %collective-permute-start.15 = (bf16[512,512]{1,0:T(8,128)(2,1)}, bf16[512,512]{1,0:T(8,128)(2,1)}, u32[]{:S(2)}, u32[]{:S(2)}) collective-permute-start(bf16[512,512]{1,0:T(8,128)(2,1)} %copy-done.63), channel_id=1, source_target_pairs={{0,2},{2,0},{4,6},{6,4},{8,10},{10,8},{12,14},{14,12},{1,3},{3,1},... | collective-permute-start | bytes 1572872 | tf_op jit(solution)/shard_map/ppermute | solution.py:229
  124.3 47.1 %collective-permute-start.44 = (bf16[512,512]{1,0:T(8,128)(2,1)}, bf16[512,512]{1,0:T(8,128)(2,1)}, u32[]{:S(2)}, u32[]{:S(2)}) collective-permute-start(bf16[512,512]{1,0:T(8,128)(2,1)} %get-tuple-element.31), channel_id=1, source_target_pairs={{0,4},{2,6},{4,8},{6,10},{8,12},{10,14},{12,0},{14,2},{1,5},{3,7},... | collective-permute-start | bytes 1572872 | tf_op jit(solution)/shard_map/ppermute | solution.py:229
  132.8 40.2 %collective-permute-start.46 = (bf16[512,512]{1,0:T(8,128)(2,1)}, bf16[512,512]{1,0:T(8,128)(2,1)}, u32[]{:S(2)}, u32[]{:S(2)}) collective-permute-start(bf16[512,512]{1,0:T(8,128)(2,1)} %get-tuple-element.31), channel_id=1, source_target_pairs={{0,12},{2,14},{4,0},{6,2},{8,4},{10,6},{12,8},{14,10},{1,13},{3,15... | collective-permute-start | bytes 1572872 | tf_op jit(solution)/shard_map/ppermute | solution.py:229
  144.2 36.8 %collective-permute-start.48 = (bf16[512,512]{1,0:T(8,128)(2,1)}, bf16[512,512]{1,0:T(8,128)(2,1)}, u32[]{:S(2)}, u32[]{:S(2)}) collective-permute-start(bf16[512,512]{1,0:T(8,128)(2,1)} %get-tuple-element.32.refs_0_), channel_id=1, source_target_pairs={{0,8},{2,10},{4,12},{6,14},{8,0},{10,2},{12,4},{14,6},{1,9},{3,11}... | collective-permute-start | bytes 1572872 | tf_op jit(solution)/shard_map/ppermute | solution.py:229
  154.6 26.6 %collective-permute-start.24 = (bf16[512,512]{1,0:T(8,128)(2,1)S(1)}, bf16[512,512]{1,0:T(8,128)(2,1)S(1)}, u32[]{:S(2)}, u32[]{:S(2)}) collective-permute-start(bf16[512,512]{1,0:T(8,128)(2,1)S(1)} %collective-permute-done.23.refs_2_), channel_id=1, source_target_pairs={{0,2},{2,0},{4,6},{6,4},{8,10},{10,8},{12,14},{14,12},{1,3},{3,1},... | collective-permute-start | bytes 1572872 | tf_op jit(solution)/shard_map/ppermute | solution.py:229
  195.8 31.9 %collective-permute-start.30 = (bf16[512,512]{1,0:T(8,128)(2,1)S(1)}, bf16[512,512]{1,0:T(8,128)(2,1)S(1)}, u32[]{:S(2)}, u32[]{:S(2)}) collective-permute-start(bf16[512,512]{1,0:T(8,128)(2,1)S(1)} %collective-permute-done.17.refs_9_.refs_2_), channel_id=1, source_target_pairs={{0,16},{16,0},{1,17},{17,1},{2,18},{18,2},{3,19},{19,3},{4,20},{20... | collective-permute-start | bytes 1572872 | tf_op jit(solution)/shard_map/ppermute | solution.py:229
  198.2 30.4 %collective-permute-start.18 = (bf16[512,512]{1,0:T(8,128)(2,1)S(1)}, bf16[512,512]{1,0:T(8,128)(2,1)S(1)}, u32[]{:S(2)}, u32[]{:S(2)}) collective-permute-start(bf16[512,512]{1,0:T(8,128)(2,1)S(1)} %collective-permute-done.17.refs_9_.refs_2_), channel_id=1, source_target_pairs={{0,1},{1,0},{2,3},{3,2},{4,5},{5,4},{6,7},{7,6},{8,9},{9,8},{10,11... | collective-permute-start | bytes 1572872 | tf_op jit(solution)/shard_map/ppermute | solution.py:229
  206.1 28.3 %collective-permute-start.37 = (bf16[512,512]{1,0:T(8,128)(2,1)S(1)}, bf16[512,512]{1,0:T(8,128)(2,1)}, u32[]{:S(2)}, u32[]{:S(2)}) collective-permute-start(bf16[512,512]{1,0:T(8,128)(2,1)S(1)} %collective-permute-done.20.refs_9_.refs_6_), channel_id=1, source_target_pairs={{0,16},{16,0},{1,17},{17,1},{2,18},{18,2},{3,19},{19,3},{4,20},{20... | collective-permute-start | bytes 1572872 | tf_op jit(solution)/shard_map/ppermute | solution.py:229
  207.6 26.8 %collective-permute-start.21 = (bf16[512,512]{1,0:T(8,128)(2,1)S(1)}, bf16[512,512]{1,0:T(8,128)(2,1)S(1)}, u32[]{:S(2)}, u32[]{:S(2)}) collective-permute-start(bf16[512,512]{1,0:T(8,128)(2,1)S(1)} %collective-permute-done.20.refs_9_.refs_6_), channel_id=1, source_target_pairs={{0,1},{1,0},{2,3},{3,2},{4,5},{5,4},{6,7},{7,6},{8,9},{9,8},{10,11... | collective-permute-start | bytes 1572872 | tf_op jit(solution)/shard_map/ppermute | solution.py:229
  229.4 29.6 %collective-permute-start.38 = (bf16[512,512]{1,0:T(8,128)(2,1)}, bf16[512,512]{1,0:T(8,128)(2,1)}, u32[]{:S(2)}, u32[]{:S(2)}) collective-permute-start(bf16[512,512]{1,0:T(8,128)(2,1)} %collective-permute-done.36.refs_10_), channel_id=1, source_target_pairs={{0,1},{1,0},{2,3},{3,2},{4,5},{5,4},{6,7},{7,6},{8,9},{9,8},{10,11... | collective-permute-start | bytes 1572872 | tf_op jit(solution)/shard_map/ppermute | solution.py:229
  234.4 35.5 %collective-permute-start.39 = (bf16[512,512]{1,0:T(8,128)(2,1)}, bf16[512,512]{1,0:T(8,128)(2,1)}, u32[]{:S(2)}, u32[]{:S(2)}) collective-permute-start(bf16[512,512]{1,0:T(8,128)(2,1)} %collective-permute-done.37.refs_12_), channel_id=1, source_target_pairs={{0,1},{1,0},{2,3},{3,2},{4,5},{5,4},{6,7},{7,6},{8,9},{9,8},{10,11... | collective-permute-start | bytes 1572872 | tf_op jit(solution)/shard_map/ppermute | solution.py:229
  235.3 49.6 %collective-permute-start.43 = (bf16[512,512]{1,0:T(8,128)(2,1)}, bf16[512,512]{1,0:T(8,128)(2,1)}, u32[]{:S(2)}, u32[]{:S(2)}) collective-permute-start(bf16[512,512]{1,0:T(8,128)(2,1)} %get-tuple-element.32.refs_0_), channel_id=1, source_target_pairs={{0,2},{2,0},{4,6},{6,4},{8,10},{10,8},{12,14},{14,12},{1,3},{3,1},... | collective-permute-start | bytes 1572872 | tf_op jit(solution)/shard_map/ppermute | solution.py:229
  237.6 47.4 %collective-permute-start.45 = (bf16[512,512]{1,0:T(8,128)(2,1)}, bf16[512,512]{1,0:T(8,128)(2,1)}, u32[]{:S(2)}, u32[]{:S(2)}) collective-permute-start(bf16[512,512]{1,0:T(8,128)(2,1)} %collective-permute-done.44.refs_2_), channel_id=1, source_target_pairs={{0,2},{2,0},{4,6},{6,4},{8,10},{10,8},{12,14},{14,12},{1,3},{3,1},... | collective-permute-start | bytes 1572872 | tf_op jit(solution)/shard_map/ppermute | solution.py:229
  238.9 48.2 %collective-permute-start.47 = (bf16[512,512]{1,0:T(8,128)(2,1)}, bf16[512,512]{1,0:T(8,128)(2,1)}, u32[]{:S(2)}, u32[]{:S(2)}) collective-permute-start(bf16[512,512]{1,0:T(8,128)(2,1)} %collective-permute-done.46.refs_4_), channel_id=1, source_target_pairs={{0,2},{2,0},{4,6},{6,4},{8,10},{10,8},{12,14},{14,12},{1,3},{3,1},... | collective-permute-start | bytes 1572872 | tf_op jit(solution)/shard_map/ppermute | solution.py:229
  259.0 28.1 %collective-permute-start.34 = (bf16[512,512]{1,0:T(8,128)(2,1)S(1)}, bf16[512,512]{1,0:T(8,128)(2,1)}, u32[]{:S(2)}, u32[]{:S(2)}) collective-permute-start(bf16[512,512]{1,0:T(8,128)(2,1)S(1)} %shard_map.19.refs_8_), channel_id=1, source_target_pairs={{0,4},{2,6},{4,0},{6,2},{8,12},{10,14},{12,8},{14,10},{1,5},{3,7},... | collective-permute-start | bytes 1572872 | tf_op jit(solution)/shard_map/ppermute | solution.py:229
  288.1 34.3 %collective-permute-start.55 = (bf16[512,512]{1,0:T(8,128)(2,1)}, bf16[512,512]{1,0:T(8,128)(2,1)}, u32[]{:S(2)}, u32[]{:S(2)}) collective-permute-start(bf16[512,512]{1,0:T(8,128)(2,1)} %shard_map.20.refs_8_.refs_12_), channel_id=1, source_target_pairs={{0,16},{16,0},{1,17},{17,1},{2,18},{18,2},{3,19},{19,3},{4,20},{20... | collective-permute-start | bytes 1572872 | tf_op jit(solution)/shard_map/ppermute | solution.py:229
  290.0 32.4 %collective-permute-start.35 = (bf16[512,512]{1,0:T(8,128)(2,1)}, bf16[512,512]{1,0:T(8,128)(2,1)S(1)}, u32[]{:S(2)}, u32[]{:S(2)}) collective-permute-start(bf16[512,512]{1,0:T(8,128)(2,1)} %collective-permute-done.34.refs_9_.refs_10_), channel_id=1, source_target_pairs={{0,1},{1,0},{2,3},{3,2},{4,5},{5,4},{6,7},{7,6},{8,9},{9,8},{10,11... | collective-permute-start | bytes 1572872 | tf_op jit(solution)/shard_map/ppermute | solution.py:229
  301.3 32.0 %collective-permute-start.56 = (bf16[512,512]{1,0:T(8,128)(2,1)}, bf16[512,512]{1,0:T(8,128)(2,1)}, u32[]{:S(2)}, u32[]{:S(2)}) collective-permute-start(bf16[512,512]{1,0:T(8,128)(2,1)} %collective-permute-done.41.refs_9_.refs_14_), channel_id=1, source_target_pairs={{0,16},{16,0},{1,17},{17,1},{2,18},{18,2},{3,19},{19,3},{4,20},{20... | collective-permute-start | bytes 1572872 | tf_op jit(solution)/shard_map/ppermute | solution.py:229
  (101 other events, 968.4 us)
